TPU v7x, 32 devices: a whole 2x2x4 slice. The times are simulated.
32 devices in a mesh: fsdp: 8 (over z, y), tp: 4 (over x, core).
Axes of the slice: x: 2, y: 2, z: 4, core: 2. Of those that a mesh axis runs over, the one named last changes fastest.
Arguments:
- layer_input: bfloat16 [8192, 768], P(('fsdp', 'tp')), may hold values from -12 to 12
- out_cotangent: bfloat16 [8192, 768], P(('fsdp', 'tp')), may hold values from -12 to 12
- segments: int32 [8, 1024], P('fsdp'), may hold values from 0 to 3, never falling along the last dimension, each value on 1 to 512 neighbouring positions
- norm_gain: float32 [768], replicated, may hold values from 0.5 to 1.5
- norm_bias: float32 [768], replicated, may hold values from -3 to 3
- qkv_weight: bfloat16 [768, 2304], P('fsdp', 'tp'), may hold values from -20 to 20
- qkv_bias: float32 [2304], P('tp'), may hold values from -3 to 3
- out_weight: bfloat16 [768, 768], P('tp', 'fsdp'), may hold values from -0.875 to 0.875
- out_bias: float32 [768], replicated, may hold values from -3 to 3
- up_weight: bfloat16 [768, 3072], P('fsdp', 'tp'), may hold values from -0.21875 to 0.21875
- up_bias: float32 [3072], P('tp'), may hold values from -3 to 3
- down_weight: bfloat16 [3072, 768], P('tp', 'fsdp'), may hold values from -0.109375 to 0.109375
- down_bias: float32 [768], replicated, may hold values from -3 to 3
Outputs:
- layer_output: bfloat16 [8192, 768], P(('fsdp', 'tp'))
- input_grad: bfloat16 [8192, 768], P(('fsdp', 'tp'))
- norm_gain_grad: float32 [768], replicated
- norm_bias_grad: float32 [768], replicated
- qkv_weight_grad: float32 [768, 2304], P('fsdp', 'tp')
- qkv_bias_grad: float32 [2304], P('tp')
- out_weight_grad: float32 [768, 768], P('tp', 'fsdp')
- out_bias_grad: float32 [768], replicated
- up_weight_grad: float32 [768, 3072], P('fsdp', 'tp')
- up_bias_grad: float32 [3072], P('tp')
- down_weight_grad: float32 [3072, 768], P('tp', 'fsdp')
- down_bias_grad: float32 [768], replicated
Inputs may be any that keep to these rules, and one draw needn't show every extreme that they name: `segments`: each row is one sequence of 1024 tokens; its numbers name documents, never fall along the row, and each document spans 1 to 512 tokens, one exactly 512.
All inputs are finite; a program needn't handle non-finite values.
Results may differ from a plain program's by a relative error of at most 0.01.
Values may be sent and summed in bfloat16 or wider, within the bound.
A program may use at most 128 MiB of HBM per device.

v0:
```python
import jax
import jax.numpy as jnp
from jax import lax
from jax.sharding import PartitionSpec as P

HEAD_DIM = 64
ROT = 16


EPSILON = 1e-05
ROTARY_BASE = 10000.0


def layer_norm(values, gain, shift):
    center = values - jnp.mean(values, axis=-1, keepdims=True)
    spread = jnp.mean(center * center, axis=-1, keepdims=True)
    inverse = lax.rsqrt(spread + EPSILON)
    normed = center * inverse
    return (normed, inverse, normed * gain + shift)


def gelu_value(pre_act):
    return 0.5 * pre_act * (1.0 + lax.erf(pre_act * 0.7071067811865476))


def gelu_slope(pre_act):
    return (
        0.5 * (1.0 + lax.erf(pre_act * 0.7071067811865476))
        + pre_act * jnp.exp(-0.5 * pre_act * pre_act) * 0.3989422804014327
    )


def positions_of(segment_row):
    length = segment_row.shape[0]
    counter = jnp.arange(length, dtype=jnp.int32)
    is_start = jnp.concatenate(
        [jnp.ones((1,), dtype=jnp.bool_), segment_row[1:] != segment_row[:-1]]
    )
    starts = lax.cummax(jnp.where(is_start, counter, jnp.zeros_like(counter)), axis=0)
    return counter - starts


def rotary_tables(positions):
    halves = ROT // 2
    inverse_freq = ROTARY_BASE ** (-(jnp.arange(halves, dtype=jnp.float32) * 2.0) / ROT)
    angles = positions.astype(jnp.float32)[:, None] * inverse_freq[None, :]
    cos_table = jnp.cos(angles)
    sin_table = jnp.sin(angles)
    return (
        jnp.concatenate([cos_table, cos_table], axis=-1),
        jnp.concatenate([sin_table, sin_table], axis=-1),
    )


def rotate(tensor, cos_table, sin_table):
    halves = ROT // 2
    turned_part = tensor[..., :ROT]
    turned = jnp.concatenate([-turned_part[..., halves:], turned_part[..., :halves]], axis=-1)
    spun = turned_part * cos_table[:, None, :] + turned * sin_table[:, None, :]
    return jnp.concatenate([spun, tensor[..., ROT:]], axis=-1)


def unrotate(grad_in, cos_table, sin_table):
    halves = ROT // 2
    turned_part = grad_in[..., :ROT]
    scaled = turned_part * sin_table[:, None, :]
    back = jnp.concatenate([scaled[..., halves:], -scaled[..., :halves]], axis=-1)
    return jnp.concatenate(
        [turned_part * cos_table[:, None, :] + back, grad_in[..., ROT:]], axis=-1
    )


def cross_rows(left, right):
    return lax.dot_general(
        left, right, (((0,), (0,)), ((), ())), preferred_element_type=jnp.float32
    )


def cross_cols(left, right):
    return lax.dot_general(
        left, right, (((1,), (1,)), ((), ())), preferred_element_type=jnp.float32
    )


def block_scores(queries, keys_in, segment_row, first_row, last_row, score_scale):
    counter = jnp.arange(last_row, dtype=jnp.int32)
    allowed = (segment_row[first_row:last_row, None] == segment_row[None, :last_row]) & (
        counter[first_row:last_row, None] >= counter[None, :last_row]
    )
    scores = cross_cols(queries[first_row:last_row], keys_in[:last_row]) * score_scale
    return jnp.where(allowed, scores, -jnp.inf)


def head_forward(queries, keys_in, values_in, segment_row, score_scale):
    length = queries.shape[0]
    span = min(512, length)
    mixed_parts = []
    total_parts = []
    for first_row in range(0, length, span):
        last_row = min(first_row + span, length)
        scores = block_scores(queries, keys_in, segment_row, first_row, last_row, score_scale)
        highest = jnp.max(scores, axis=-1, keepdims=True)
        log_total = highest + jnp.log(jnp.sum(jnp.exp(scores - highest), axis=-1, keepdims=True))
        weights = jnp.exp(scores - log_total).astype(jnp.bfloat16)
        mixed_parts.append(
            jnp.dot(weights, values_in[:last_row], preferred_element_type=jnp.float32).astype(
                jnp.bfloat16
            )
        )
        total_parts.append(log_total)
    return (jnp.concatenate(mixed_parts, axis=0), jnp.concatenate(total_parts, axis=0))


def head_backward(
    queries, keys_in, values_in, mixed, grad_mixed, log_total, segment_row, score_scale
):
    length = queries.shape[0]
    span = min(512, length)
    delta = jnp.sum(
        grad_mixed.astype(jnp.float32) * mixed.astype(jnp.float32), axis=-1, keepdims=True
    )
    grad_keys = jnp.zeros(keys_in.shape, jnp.float32)
    grad_values = jnp.zeros(values_in.shape, jnp.float32)
    query_parts = []
    for first_row in range(0, length, span):
        last_row = min(first_row + span, length)
        padding = ((0, length - last_row), (0, 0))
        scores = block_scores(queries, keys_in, segment_row, first_row, last_row, score_scale)
        probs = jnp.exp(scores - log_total[first_row:last_row])
        weights = probs.astype(jnp.bfloat16)
        grad_rows = grad_mixed[first_row:last_row]
        grad_values = grad_values + jnp.pad(cross_rows(weights, grad_rows), padding)
        grad_probs = cross_cols(grad_rows, values_in[:last_row])
        grad_scores = (probs * (grad_probs - delta[first_row:last_row]) * score_scale).astype(
            jnp.bfloat16
        )
        query_parts.append(
            jnp.dot(grad_scores, keys_in[:last_row], preferred_element_type=jnp.float32)
        )
        grad_keys = grad_keys + jnp.pad(
            cross_rows(grad_scores, queries[first_row:last_row]), padding
        )
    return (jnp.concatenate(query_parts, axis=0), grad_keys, grad_values)


def body(
    layer_input,
    out_cotangent,
    segments,
    norm_gain,
    norm_bias,
    qkv_weight,
    qkv_bias,
    out_weight,
    out_bias,
    up_weight,
    up_bias,
    down_weight,
    down_bias,
):
    score_scale = HEAD_DIM ** (-0.5)
    own_rows = layer_input.astype(jnp.float32)
    normed, inverse, shifted = layer_norm(own_rows, norm_gain, norm_bias)
    features = lax.all_gather(shifted.astype(jnp.bfloat16), "tp", axis=0, tiled=True)
    length = features.shape[0]
    full_qkv, full_out, full_up, full_down = (
        lax.all_gather(qkv_weight, "fsdp", axis=0, tiled=True),
        lax.all_gather(out_weight, "fsdp", axis=1, tiled=True),
        lax.all_gather(up_weight, "fsdp", axis=0, tiled=True),
        lax.all_gather(down_weight, "fsdp", axis=1, tiled=True),
    )
    local_heads = full_qkv.shape[1] // (3 * HEAD_DIM)
    segment_row = segments[0]
    cos_table, sin_table = rotary_tables(positions_of(segment_row))
    packed = (jnp.dot(features, full_qkv, preferred_element_type=jnp.float32) + qkv_bias).reshape(
        length, local_heads, 3, HEAD_DIM
    )
    queries = rotate(packed[:, :, 0], cos_table, sin_table).astype(jnp.bfloat16).transpose(1, 0, 2)
    keys_all = rotate(packed[:, :, 1], cos_table, sin_table).astype(jnp.bfloat16).transpose(1, 0, 2)
    values_all = packed[:, :, 2].astype(jnp.bfloat16).transpose(1, 0, 2)

    def forward_head(member):
        return head_forward(member[0], member[1], member[2], segment_row, score_scale)

    mixed, log_total = lax.map(forward_head, (queries, keys_all, values_all))
    mixed_rows = mixed.transpose(1, 0, 2).reshape(length, local_heads * HEAD_DIM)
    pre_act = jnp.dot(features, full_up, preferred_element_type=jnp.float32) + up_bias
    gelu_rows = gelu_value(pre_act).astype(jnp.bfloat16)
    partial_value = jnp.dot(mixed_rows, full_out, preferred_element_type=jnp.float32) + jnp.dot(
        gelu_rows, full_down, preferred_element_type=jnp.float32
    )
    branch = lax.psum_scatter(partial_value, "tp", scatter_dimension=0, tiled=True)
    layer_output = (own_rows + branch + out_bias + down_bias).astype(jnp.bfloat16)
    grad_rows = lax.all_gather(out_cotangent, "tp", axis=0, tiled=True)
    back_qkv, back_out, back_up, back_down = (full_qkv, full_out, full_up, full_down)
    down_grad = cross_rows(gelu_rows, grad_rows)
    grad_pre = cross_cols(grad_rows, back_down) * gelu_slope(pre_act)
    pre_grads = grad_pre.astype(jnp.bfloat16)
    up_grad = cross_rows(features, pre_grads)
    up_bias_part = jnp.sum(grad_pre, axis=0)
    feature_grad = cross_cols(pre_grads, back_up)
    out_grad = cross_rows(mixed_rows, grad_rows)
    mixed_grad = (
        cross_cols(grad_rows, back_out)
        .astype(jnp.bfloat16)
        .reshape(length, local_heads, HEAD_DIM)
        .transpose(1, 0, 2)
    )

    def backward_head(member):
        return head_backward(
            member[0],
            member[1],
            member[2],
            member[3],
            member[4],
            member[5],
            segment_row,
            score_scale,
        )

    grad_q, grad_k, grad_v = lax.map(
        backward_head, (queries, keys_all, values_all, mixed, mixed_grad, log_total)
    )
    grad_q = unrotate(grad_q.transpose(1, 0, 2), cos_table, sin_table)
    grad_k = unrotate(grad_k.transpose(1, 0, 2), cos_table, sin_table)
    grad_v = grad_v.transpose(1, 0, 2)
    packed_grad = jnp.stack([grad_q, grad_k, grad_v], axis=2).reshape(
        length, 3 * local_heads * HEAD_DIM
    )
    qkv_bias_part = jnp.sum(packed_grad, axis=0)
    packed_bf = packed_grad.astype(jnp.bfloat16)
    qkv_grad = cross_rows(features, packed_bf)
    feature_grad = feature_grad + cross_cols(packed_bf, back_qkv)
    qkv_grad, out_grad, up_grad, down_grad = (
        lax.psum_scatter(qkv_grad, "fsdp", scatter_dimension=0, tiled=True),
        lax.psum_scatter(out_grad, "fsdp", scatter_dimension=1, tiled=True),
        lax.psum_scatter(up_grad, "fsdp", scatter_dimension=0, tiled=True),
        lax.psum_scatter(down_grad, "fsdp", scatter_dimension=1, tiled=True),
    )
    row_grad = lax.psum_scatter(feature_grad, "tp", scatter_dimension=0, tiled=True)
    cot_rows = out_cotangent.astype(jnp.float32)
    gain_grad, shift_grad, bias_grad = lax.psum(
        (jnp.sum(row_grad * normed, axis=0), jnp.sum(row_grad, axis=0), jnp.sum(cot_rows, axis=0)),
        ("fsdp", "tp"),
    )
    qkv_bias_grad, up_bias_grad = lax.psum((qkv_bias_part, up_bias_part), "fsdp")
    scaled = row_grad * norm_gain
    input_grad = (
        cot_rows
        + inverse
        * (
            scaled
            - jnp.mean(scaled, axis=-1, keepdims=True)
            - normed * jnp.mean(scaled * normed, axis=-1, keepdims=True)
        )
    ).astype(jnp.bfloat16)
    return (
        layer_output,
        input_grad,
        gain_grad,
        shift_grad,
        qkv_grad,
        qkv_bias_grad,
        out_grad,
        bias_grad,
        up_grad,
        up_bias_grad,
        down_grad,
        bias_grad,
    )


def solution(mesh):
    in_specs = (
        P(("fsdp", "tp"), None),
        P(("fsdp", "tp"), None),
        P("fsdp", None),
        P(),
        P(),
        P("fsdp", "tp"),
        P("tp"),
        P("tp", "fsdp"),
        P(),
        P("fsdp", "tp"),
        P("tp"),
        P("tp", "fsdp"),
        P(),
    )
    out_specs = (
        P(("fsdp", "tp"), None),
        P(("fsdp", "tp"), None),
        P(),
        P(),
        P("fsdp", "tp"),
        P("tp"),
        P("tp", "fsdp"),
        P(),
        P("fsdp", "tp"),
        P("tp"),
        P("tp", "fsdp"),
        P(),
    )
    return jax.shard_map(body, mesh=mesh, in_specs=in_specs, out_specs=out_specs, check_vma=False)
```

profile of v0, /device:TPU:0, one launch (start us, length us, event | category | flops | bytes accessed | tf_op | source)
XLA Modules:
  0.0 530.0 jit_solution(7264286757015813341)
XLA Ops:
  9.7 2.0 fusion.64
  13.9 34.6 %all_gather.19 = bf16[768,576]{1,0:T(8,128)(2,1)S(1)} all-gather(bf16[96,576]{1,0:T(8,128)(2,1)S(1)} %copy-done.11), channel_id=1, replica_groups=mesh['fsdp'=8,'tp'=4] {'fsdp'}, dimensions={0}, use_global_device_ids=true | all-gather | bytes 995328 | tf_op jit(solution)/shard_map/all_gather | solution.py:167
  49.3 31.3 %all_gather.20 = bf16[192,768]{0,1:T(8,128)(2,1)S(1)} all-gather(bf16[192,96]{0,1:T(8,128)(2,1)S(1)} %copy.81), channel_id=1, replica_groups=mesh['fsdp'=8,'tp'=4] {'fsdp'}, dimensions={1}, use_global_device_ids=true | all-gather | bytes 331776 | tf_op jit(solution)/shard_map/all_gather | solution.py:168
  80.9 2.5 convolution_add_fusion.4
  86.6 16.1 %while.28 = (s32[]{:T(128)}, bf16[3,1024,64]{1,2,0:T(8,128)(2,1)}, f32[3,1024,1]{1,2,0:T(1,128)S(1)}, s32[1024]{0:T(1024)S(1)}, bf16[3,1024,64]{2,1,0:T(8,128)(2...) while((s32[]{:T(128)}, bf16[3,1024,64]{1,2,0:T(8,128)(2,1)}, ...), condition=%wide.region_9.10_spmd, body=%wide.region_4.9_spmd.sunk | while | flops 209518592 | bytes 10947209 | solution.py:185
  88.2 1.8 fusion.151
  102.7 2.1 convolution_convert_fusion.2
  106.0 45.1 %while.29 = (s32[]{:T(128)}, f32[3,1024,64]{1,2,0:T(8,128)}, f32[3,1024,64]{1,2,0:T(8,128)}, f32[3,1024,64]{1,2,0:T(8,128)}, s32[1024]{0:T(1024)S(1)}, /*index=5...) while((s32[]{:T(128)}, f32[3,1024,64]{1,2,0:T(8,128)}, ...), condition=%wide.region_13.14_spmd, body=%wide.region_11.13_spmd.sunk | while | flops 512424960 | bytes 20644056 | solution.py:222
  106.0 1.8 subtract_exponential_fusion.2
  114.4 2.0 fusion.172
  121.0 1.8 subtract_exponential_fusion.2
  129.5 2.0 fusion.172
  136.1 1.8 subtract_exponential_fusion.2
  144.5 2.0 fusion.172
  158.2 2.6 convolution_bitcast_fusion
  161.1 5.4 %multiply_convert_fusion.1 = (bf16[1024,768]{1,0:T(8,128)(2,1)}, f32[1024,768]{1,0:T(8,128)}) fusion(f32[768]{0:T(1024)S(1)} %copy-done.19, bf16[1024,768]{1,0:T(8,128)(2,1)} %all-gather.5.cloned.1.call-done, bf16[768,768]{1,0:T(8,128)(2,1)} %all-gather.7.cloned.1.call-done), kind=kOutput, calls=%fused_computation.93 | convolution fusion | flops 1212678144 | bytes 7474176 | tf_op jit(solution)/shard_map/dot_general | solution.py:187
  166.5 4.1 fusion.91
  172.8 3.1 convolution_add_fusion.2
  176.0 3.2 fusion.92
  179.3 3.3 convolution_add_fusion.3
  182.7 4.5 fusion.93
  187.2 4.8 fusion.74
  192.1 4.3 fusion.94
  197.9 22.1 %all-reduce.3 = (f32[576]{0:T(1024)}, f32[768]{0:T(1024)}) all-reduce(f32[576]{0:T(1024)S(1)} %reduce_sum.120, f32[768]{0:T(1024)S(1)} %get-tuple-element.415), channel_id=1, replica_groups=mesh['fsdp'=8,'tp'=4] {'fsdp'}, use_global_device_ids=true, to_apply=%region_23.24 | all-reduce | flops 1344 | bytes 10752 | tf_op jit(solution)/shard_map/psum | solution.py:247
  220.1 5.1 reduce-scatter.19.cloned.1.call-done
  226.8 37.7 %reduce-scatter.11.cloned.1.call-done = f32[256,768]{1,0:T(8,128)} async-done(((f32[1024,768]{1,0:T(8,128)}), f32[256,768]{1,0:T(8,128)}) %reduce-scatter.11.cloned.1.call-update) | async-done | bytes 786448 | tf_op jit(solution)/shard_map/reduce_scatter | solution.py:241
  266.0 38.9 %reduce-scatter.9.cloned.1.call-done = f32[256,768]{1,0:T(8,128)} async-done(((f32[1024,768]{1,0:T(8,128)}), f32[256,768]{1,0:T(8,128)}) %reduce-scatter.9.cloned.1.call-update) | async-done | bytes 786448 | tf_op jit(solution)/shard_map/reduce_scatter | solution.py:192
  304.9 2.6 convert_reduce_fusion.1
  307.6 40.2 %all-reduce.2 = (f32[768]{0:T(1024)}, f32[768]{0:T(1024)}, f32[768]{0:T(1024)S(1)}) all-reduce(f32[768]{0:T(1024)S(1)} %get-tuple-element.331, f32[768]{0:T(1024)S(1)} %get-tuple-element.334, f32[768]{0:T(1024)S(1)} %get-tuple-element.398), channel_id=1, replica_groups=mesh['fsdp'=8,'tp'=4] {'fsdp','tp'}, use_global_device_ids=true, to_apply=%region_18.19 | all-reduce | flops 2304 | bytes 18432 | tf_op jit(solution)/shard_map/psum | solution.py:243
  347.8 28.9 %reduce-scatter.13.cloned.1.call-done = f32[96,576]{1,0:T(8,128)} async-done(((f32[768,576]{1,0:T(8,128)}), f32[96,576]{1,0:T(8,128)}) %reduce-scatter.13.cloned.1.call-update) | async-done | bytes 221200 | tf_op jit(solution)/shard_map/reduce_scatter | solution.py:236
  376.7 73.0 %reduce-scatter.15.cloned.1.call-done = f32[96,768]{1,0:T(8,128)} async-done(((f32[768,768]{1,0:T(8,128)}), f32[96,768]{1,0:T(8,128)}) %reduce-scatter.15.cloned.1.call-update) | async-done | bytes 294928 | tf_op jit(solution)/shard_map/reduce_scatter | solution.py:238
  449.7 72.9 %reduce-scatter.17.cloned.1.call-done = f32[768,96]{0,1:T(8,128)} async-done(((f32[768,768]{0,1:T(8,128)}), f32[768,96]{0,1:T(8,128)}) %reduce-scatter.17.cloned.1.call-update) | async-done | bytes 294928 | tf_op jit(solution)/shard_map/reduce_scatter | solution.py:239
  (210 shorter events, 72.5 us)
Async XLA Ops:
  7.2 6.7 %copy-start.11 = (bf16[96,576]{1,0:T(8,128)(2,1)S(1)}, bf16[96,576]{1,0:T(8,128)(2,1)}, u32[]{:S(2)}) copy-start(bf16[96,576]{1,0:T(8,128)(2,1)} %param.22) | copy-start | bytes 331780
  7.2 41.3 %copy-start.10 = (s32[1,1024]{1,0:T(1,128)S(1)}, s32[1,1024]{1,0:T(1,128)}, u32[]{:S(2)}) copy-start(s32[1,1024]{1,0:T(1,128)} %param.19) | copy-start | bytes 12292
  7.2 42.0 %copy-start.12 = (bf16[192,96]{1,0:T(8,128)(2,1)S(1)}, bf16[192,96]{1,0:T(8,128)(2,1)}, u32[]{:S(2)}) copy-start(bf16[192,96]{1,0:T(8,128)(2,1)} %param.24) | copy-start | bytes 110596
  7.2 73.7 %all-gather.5.cloned.1.call-start = ((), (), s32[]{:S(2)}) async-start(), calls=%async_computation.6 | async-start | bytes 1966080 | tf_op jit(solution)/shard_map/all_gather | solution.py:164
  8.4 72.5 %copy-start.18 = (f32[576]{0:T(1024)S(1)}, f32[576]{0:T(1024)}, u32[]{:S(2)}) copy-start(f32[576]{0:T(1024)} %param.23) | copy-start | bytes 6916
  11.7 91.0 %all-gather.11.cloned.1.call-start = ((), (), s32[]{:S(2)}) async-start(), calls=%async_computation.10 | async-start | bytes 1966080 | tf_op jit(solution)/shard_map/all_gather | solution.py:194
  12.5 148.6 %all-gather.7.cloned.1.call-start = ((), (), s32[]{:S(2)}) async-start(), calls=%async_computation.7 | async-start | bytes 1327104 | tf_op jit(solution)/shard_map/all_gather | solution.py:169
  13.2 153.3 %all-gather.9.cloned.1.call-start = ((), (), s32[]{:S(2)}) async-start(), calls=%async_computation.8 | async-start | bytes 1327104 | tf_op jit(solution)/shard_map/all_gather | solution.py:170
  13.8 211.3 %reduce-scatter.19.cloned.1.call-start = ((), (), s32[]{:S(2)}) async-start(), calls=%async_computation.15 | async-start | bytes 884736
  48.5 35.0 %copy-start.4 = (bf16[768,576]{1,0:T(8,128)(2,1)}, bf16[768,576]{1,0:T(8,128)(2,1)S(1)}, u32[]{:S(2)}) copy-start(bf16[768,576]{1,0:T(8,128)(2,1)S(1)} %all_gather.19) | copy-start | bytes 2654212
  80.6 22.1 %copy-start.6 = (bf16[192,768]{0,1:T(8,128)(2,1)}, bf16[192,768]{0,1:T(8,128)(2,1)S(1)}, u32[]{:S(2)}) copy-start(bf16[192,768]{0,1:T(8,128)(2,1)S(1)} %all_gather.20) | copy-start | bytes 884740
  110.1 2.8 copy-start
  125.1 2.8 copy-start
  140.2 2.8 copy-start
  151.1 2.3 copy-start.9
  155.5 2.6 copy-start.2
  158.2 2.9 copy-start.19
  160.8 103.7 %reduce-scatter.11.cloned.1.call-start = ((), (), s32[]{:S(2)}) async-start(), calls=%async_computation.11 | async-start | bytes 3932160 | tf_op jit(solution)/shard_map/reduce_scatter | solution.py:241
  166.5 4.2 copy-start.17
  170.7 1.8 copy-start.3
  170.7 2.1 copy-start.5
  175.9 129.0 %reduce-scatter.9.cloned.1.call-start = ((), (), s32[]{:S(2)}) async-start(), calls=%async_computation.9 | async-start | bytes 3932160 | tf_op jit(solution)/shard_map/reduce_scatter | solution.py:192
  176.0 3.2 copy-start.7
  182.6 194.1 %reduce-scatter.13.cloned.1.call-start = ((), (), s32[]{:S(2)}) async-start(), calls=%async_computation.12 | async-start | bytes 2211840 | tf_op jit(solution)/shard_map/reduce_scatter | solution.py:236
  187.2 262.5 %reduce-scatter.15.cloned.1.call-start = ((), (), s32[]{:S(2)}) async-start(), calls=%async_computation.13 | async-start | bytes 2654208 | tf_op jit(solution)/shard_map/reduce_scatter | solution.py:238
  192.0 330.5 %reduce-scatter.17.cloned.1.call-start = ((), (), s32[]{:S(2)}) async-start(), calls=%async_computation.14 | async-start | bytes 2654208 | tf_op jit(solution)/shard_map/reduce_scatter | solution.py:239
  196.4 68.1 %copy-start.1 = (bf16[256,768]{1,0:T(8,128)(2,1)S(1)}, bf16[256,768]{1,0:T(8,128)(2,1)}, u32[]{:S(2)}) copy-start(bf16[256,768]{1,0:T(8,128)(2,1)} %param.17) | copy-start | bytes 1179652
  196.4 68.1 %copy-start.13 = (f32[768]{0:T(1024)S(1)}, f32[768]{0:T(1024)}, u32[]{:S(2)}) copy-start(f32[768]{0:T(1024)} %param.20) | copy-start | bytes 9220
  196.4 108.5 %copy-start.8 = (bf16[256,768]{1,0:T(8,128)(2,1)S(1)}, bf16[256,768]{1,0:T(8,128)(2,1)}, u32[]{:S(2)}) copy-start(bf16[256,768]{1,0:T(8,128)(2,1)} %param.18) | copy-start | bytes 1179652
  196.4 108.5 %copy-start.14 = (f32[768]{0:T(1024)S(1)}, f32[768]{0:T(1024)}, u32[]{:S(2)}) copy-start(f32[768]{0:T(1024)} %param.29) | copy-start | bytes 9220
  196.5 108.5 %copy-start.15 = (f32[768]{0:T(1024)S(1)}, f32[768]{0:T(1024)}, u32[]{:S(2)}) copy-start(f32[768]{0:T(1024)} %param.25) | copy-start | bytes 9220
  347.8 175.4 %copy-start.16 = (f32[768]{0:T(1024)}, f32[768]{0:T(1024)S(1)}, u32[]{:S(2)}) copy-start(f32[768]{0:T(1024)S(1)} %get-tuple-element.670) | copy-start | bytes 9220
  (1 other events, 1.5 us)
Sparse Core Ops, SparseCore 0:
  11.8 22.3 all-gather.4
  35.8 19.6 all-gather.10
  57.7 41.2 all-gather.6
  101.0 40.0 all-gather.8
  160.9 64.1 reduce-scatter.18
  227.5 36.8 reduce-scatter.10
  267.0 37.8 reduce-scatter.8
  309.0 67.6 reduce-scatter.12
  380.8 68.8 reduce-scatter.14
  453.6 68.9 reduce-scatter.16
where the time goes:
time: 531 us; the launch traced here: 530 us
  waiting for transfers between devices  258 us (49%)
  blocking collectives  128 us (24%)
  matrix products  89.1 us (17%)
  other arithmetic  24.5 us (5%)
  between operations  14.6 us (3%)
  local copies, waits for them, and re-layouts  14.2 us (3%)
    reduce_scatter x1, waiting for transfers between devices, body(): lax.psum_scatter(up_grad, 'fsdp', scatter_dimension=0, tiled=True)  73 us
    reduce_scatter x1, waiting for transfers between devices, body(): lax.psum_scatter(down_grad, 'fsdp', scatter_dimension=1, tiled=True)  72.9 us
    psum x1, blocking collectives, body(): lax.psum((jnp.sum(row_grad * normed, axis=0), jnp.sum(row_grad, axis=0),...  40.2 us
    reduce_scatter x1, waiting for transfers between devices, body(): lax.psum_scatter(partial_value, 'tp', scatter_dimension=0, tiled=True)  38.9 us
    reduce_scatter x1, waiting for transfers between devices, body(): lax.psum_scatter(feature_grad, 'tp', scatter_dimension=0, tiled=True)  37.7 us
    dot_general x22, matrix products, cross_cols(): lax.dot_general(left, right, (((1,), (1,)), ((), ())), preferred_element_...  34.8 us
    all_gather x1, blocking collectives, body(): lax.all_gather(qkv_weight, 'fsdp', axis=0, tiled=True)  34.6 us
    all_gather x1, blocking collectives, body(): lax.all_gather(out_weight, 'fsdp', axis=1, tiled=True)  31.3 us
  transfers between devices with their start and end apart: 10, of which 6 were waited for; matrix products, arithmetic and copies ran while one was open for 23% of the time, Pallas kernels for 0%

commit v1 on v0

--- a/solution.py
+++ b/solution.py
@@ -1,6 +1,10 @@
+import functools
+
 import jax
 import jax.numpy as jnp
 from jax import lax
+from jax.experimental import pallas as pl
+from jax.experimental.pallas import tpu as pltpu
 from jax.sharding import PartitionSpec as P
 
 HEAD_DIM = 64
@@ -143,6 +147,153 @@
     return (jnp.concatenate(query_parts, axis=0), grad_keys, grad_values)
 
 
+MESH = pl.DeviceIdType.MESH
+
+
+def vector_sums(fsdp, tp, all_rows, rows_ref, out_ref, first, second, send, recv, send2, recv2):
+    f = lax.axis_index("fsdp")
+    t = lax.axis_index("tp")
+    barrier = pltpu.get_barrier_semaphore()
+
+    def greet_f(step, carry):
+        pl.semaphore_signal(
+            barrier, inc=1, device_id=(lax.rem(f + step, fsdp), t), device_id_type=MESH
+        )
+        return carry
+
+    def greet_t(step, carry):
+        pl.semaphore_signal(
+            barrier, inc=1, device_id=(f, lax.rem(t + step, tp)), device_id_type=MESH
+        )
+        return carry
+
+    lax.fori_loop(1, fsdp, greet_f, 0)
+    lax.fori_loop(1, tp, greet_t, 0)
+    pl.semaphore_wait(barrier, fsdp + tp - 2)
+
+    def copy_f(step, source):
+        return pltpu.make_async_remote_copy(
+            src_ref=rows_ref,
+            dst_ref=first.at[source],
+            send_sem=send.at[step],
+            recv_sem=recv.at[step],
+            device_id=(lax.rem(f + step, fsdp), t),
+            device_id_type=MESH,
+        )
+
+    def start_f(step, carry):
+        copy_f(step, f).start()
+        return carry
+
+    def wait_f(step, carry):
+        copy_f(step, lax.rem(f + fsdp - step, fsdp)).wait()
+        return carry
+
+    lax.fori_loop(1, fsdp, start_f, 0)
+    first[f] = rows_ref[...]
+    lax.fori_loop(1, fsdp, wait_f, 0)
+    total = lax.fori_loop(
+        1, fsdp, lambda step, value: value + first[step], first[0]
+    )
+    second[t] = total[:all_rows]
+
+    def copy_t(step, source):
+        return pltpu.make_async_remote_copy(
+            src_ref=second.at[t],
+            dst_ref=second.at[source],
+            send_sem=send2.at[step],
+            recv_sem=recv2.at[step],
+            device_id=(f, lax.rem(t + step, tp)),
+            device_id_type=MESH,
+        )
+
+    for step in range(1, tp):
+        copy_t(step, t).start()
+    for step in range(1, tp):
+        copy_t(step, lax.rem(t + tp - step, tp)).wait()
+    whole = second[0]
+    for step in range(1, tp):
+        whole = whole + second[step]
+    out_ref[:all_rows] = whole
+    out_ref[all_rows:] = total[all_rows:]
+
+
+def sum_vectors(rows, all_rows):
+    fsdp = lax.axis_size("fsdp")
+    tp = lax.axis_size("tp")
+    return pl.pallas_call(
+        functools.partial(vector_sums, fsdp, tp, all_rows),
+        out_shape=jax.ShapeDtypeStruct(rows.shape, jnp.float32),
+        in_specs=[pl.BlockSpec(memory_space=pltpu.VMEM)],
+        out_specs=pl.BlockSpec(memory_space=pltpu.VMEM),
+        scratch_shapes=[
+            pltpu.VMEM((fsdp,) + rows.shape, jnp.float32),
+            pltpu.VMEM((tp, all_rows, rows.shape[1]), jnp.float32),
+            pltpu.SemaphoreType.DMA((fsdp,)),
+            pltpu.SemaphoreType.DMA((fsdp,)),
+            pltpu.SemaphoreType.DMA((tp,)),
+            pltpu.SemaphoreType.DMA((tp,)),
+        ],
+        compiler_params=pltpu.CompilerParams(collective_id=1, has_side_effects=True),
+        name="vector_sums",
+    )(rows)
+
+
+def gather_weights(shard):
+    return lax.all_gather(shard, "fsdp", axis=0, tiled=True)
+
+
+def scatter_grads(grads):
+    return lax.psum_scatter(
+        grads.astype(jnp.bfloat16), "fsdp", scatter_dimension=0, tiled=True
+    )
+
+
+def scatter_rows(partial):
+    return lax.psum_scatter(
+        partial.astype(jnp.bfloat16), "tp", scatter_dimension=0, tiled=True
+    ).astype(jnp.float32)
+
+
+def attention_branch(features, grad_rows, qkv_full, qkv_bias, out_full, segment_row):
+    score_scale = HEAD_DIM ** (-0.5)
+    length = features.shape[0]
+    local_heads = qkv_full.shape[1] // (3 * HEAD_DIM)
+    cos_table, sin_table = rotary_tables(positions_of(segment_row))
+    packed = (jnp.dot(features, qkv_full, preferred_element_type=jnp.float32) + qkv_bias).reshape(
+        length, local_heads, 3, HEAD_DIM
+    )
+    queries = rotate(packed[:, :, 0], cos_table, sin_table).astype(jnp.bfloat16).transpose(1, 0, 2)
+    keys_all = rotate(packed[:, :, 1], cos_table, sin_table).astype(jnp.bfloat16).transpose(1, 0, 2)
+    values_all = packed[:, :, 2].astype(jnp.bfloat16).transpose(1, 0, 2)
+
+    def forward_head(member):
+        return head_forward(member[0], member[1], member[2], segment_row, score_scale)
+
+    mixed, log_total = lax.map(forward_head, (queries, keys_all, values_all))
+    mixed_rows = mixed.transpose(1, 0, 2).reshape(length, local_heads * HEAD_DIM)
+    mixed_grad = (
+        jnp.dot(grad_rows, out_full, preferred_element_type=jnp.float32)
+        .astype(jnp.bfloat16)
+        .reshape(length, local_heads, HEAD_DIM)
+        .transpose(1, 0, 2)
+    )
+
+    def backward_head(member):
+        return head_backward(*member, segment_row, score_scale)
+
+    grad_q, grad_k, grad_v = lax.map(
+        backward_head, (queries, keys_all, values_all, mixed, mixed_grad, log_total)
+    )
+    grad_q = unrotate(grad_q.transpose(1, 0, 2), cos_table, sin_table)
+    grad_k = unrotate(grad_k.transpose(1, 0, 2), cos_table, sin_table)
+    grad_v = grad_v.transpose(1, 0, 2)
+    packed_grad = jnp.stack([grad_q, grad_k, grad_v], axis=2).reshape(
+        length, 3 * local_heads * HEAD_DIM
+    )
+    return mixed_rows, packed_grad.astype(jnp.bfloat16), jnp.sum(packed_grad, axis=0)
+
+
 def body(
     layer_input,
     out_cotangent,
@@ -158,93 +309,73 @@
     down_weight,
     down_bias,
 ):
-    score_scale = HEAD_DIM ** (-0.5)
+    width_qkv = qkv_weight.shape[1]
+    width_out = out_weight.shape[0]
+    width_up = up_weight.shape[1]
     own_rows = layer_input.astype(jnp.float32)
     normed, inverse, shifted = layer_norm(own_rows, norm_gain, norm_bias)
     features = lax.all_gather(shifted.astype(jnp.bfloat16), "tp", axis=0, tiled=True)
-    length = features.shape[0]
-    full_qkv, full_out, full_up, full_down = (
-        lax.all_gather(qkv_weight, "fsdp", axis=0, tiled=True),
-        lax.all_gather(out_weight, "fsdp", axis=1, tiled=True),
-        lax.all_gather(up_weight, "fsdp", axis=0, tiled=True),
-        lax.all_gather(down_weight, "fsdp", axis=1, tiled=True),
-    )
-    local_heads = full_qkv.shape[1] // (3 * HEAD_DIM)
-    segment_row = segments[0]
-    cos_table, sin_table = rotary_tables(positions_of(segment_row))
-    packed = (jnp.dot(features, full_qkv, preferred_element_type=jnp.float32) + qkv_bias).reshape(
-        length, local_heads, 3, HEAD_DIM
-    )
-    queries = rotate(packed[:, :, 0], cos_table, sin_table).astype(jnp.bfloat16).transpose(1, 0, 2)
-    keys_all = rotate(packed[:, :, 1], cos_table, sin_table).astype(jnp.bfloat16).transpose(1, 0, 2)
-    values_all = packed[:, :, 2].astype(jnp.bfloat16).transpose(1, 0, 2)
-
-    def forward_head(member):
-        return head_forward(member[0], member[1], member[2], segment_row, score_scale)
-
-    mixed, log_total = lax.map(forward_head, (queries, keys_all, values_all))
-    mixed_rows = mixed.transpose(1, 0, 2).reshape(length, local_heads * HEAD_DIM)
+    mlp_full = gather_weights(jnp.concatenate([up_weight, down_weight.T], axis=1))
+    grad_rows = lax.all_gather(out_cotangent, "tp", axis=0, tiled=True)
+    att_full = gather_weights(jnp.concatenate([qkv_weight, out_weight.T], axis=1))
+    full_up, full_down = mlp_full[:, :width_up], mlp_full[:, width_up:]
+    full_qkv, full_out = att_full[:, :width_qkv], att_full[:, width_qkv:]
+
     pre_act = jnp.dot(features, full_up, preferred_element_type=jnp.float32) + up_bias
     gelu_rows = gelu_value(pre_act).astype(jnp.bfloat16)
-    partial_value = jnp.dot(mixed_rows, full_out, preferred_element_type=jnp.float32) + jnp.dot(
-        gelu_rows, full_down, preferred_element_type=jnp.float32
-    )
-    branch = lax.psum_scatter(partial_value, "tp", scatter_dimension=0, tiled=True)
+    grad_pre = jnp.dot(grad_rows, full_down, preferred_element_type=jnp.float32) * gelu_slope(
+        pre_act
+    )
+    pre_grads = grad_pre.astype(jnp.bfloat16)
+    up_bias_part = jnp.sum(grad_pre, axis=0)
+    mlp_grad = jnp.concatenate(
+        [
+            cross_rows(features, pre_grads).astype(jnp.bfloat16),
+            cross_rows(grad_rows, gelu_rows).astype(jnp.bfloat16),
+        ],
+        axis=1,
+    )
+    features_late, grad_late, mlp_grad, pre_grads = lax.optimization_barrier(
+        (features, grad_rows, mlp_grad, pre_grads)
+    )
+    mlp_sum = scatter_grads(mlp_grad)
+    mixed_rows, packed_bf, qkv_bias_part = attention_branch(
+        features_late, grad_late, full_qkv, qkv_bias, full_out, segments[0]
+    )
+    partial_value = cross_cols(mixed_rows, full_out) + cross_cols(gelu_rows, full_down)
+    branch = scatter_rows(partial_value)
+    feature_grad = cross_cols(packed_bf, full_qkv) + cross_cols(pre_grads, full_up)
+    row_grad = scatter_rows(feature_grad)
+    att_grad = jnp.concatenate(
+        [
+            cross_rows(features, packed_bf).astype(jnp.bfloat16),
+            cross_rows(grad_rows, mixed_rows).astype(jnp.bfloat16),
+        ],
+        axis=1,
+    )
+    att_sum = scatter_grads(att_grad)
     layer_output = (own_rows + branch + out_bias + down_bias).astype(jnp.bfloat16)
-    grad_rows = lax.all_gather(out_cotangent, "tp", axis=0, tiled=True)
-    back_qkv, back_out, back_up, back_down = (full_qkv, full_out, full_up, full_down)
-    down_grad = cross_rows(gelu_rows, grad_rows)
-    grad_pre = cross_cols(grad_rows, back_down) * gelu_slope(pre_act)
-    pre_grads = grad_pre.astype(jnp.bfloat16)
-    up_grad = cross_rows(features, pre_grads)
-    up_bias_part = jnp.sum(grad_pre, axis=0)
-    feature_grad = cross_cols(pre_grads, back_up)
-    out_grad = cross_rows(mixed_rows, grad_rows)
-    mixed_grad = (
-        cross_cols(grad_rows, back_out)
-        .astype(jnp.bfloat16)
-        .reshape(length, local_heads, HEAD_DIM)
-        .transpose(1, 0, 2)
-    )
-
-    def backward_head(member):
-        return head_backward(
-            member[0],
-            member[1],
-            member[2],
-            member[3],
-            member[4],
-            member[5],
-            segment_row,
-            score_scale,
-        )
-
-    grad_q, grad_k, grad_v = lax.map(
-        backward_head, (queries, keys_all, values_all, mixed, mixed_grad, log_total)
-    )
-    grad_q = unrotate(grad_q.transpose(1, 0, 2), cos_table, sin_table)
-    grad_k = unrotate(grad_k.transpose(1, 0, 2), cos_table, sin_table)
-    grad_v = grad_v.transpose(1, 0, 2)
-    packed_grad = jnp.stack([grad_q, grad_k, grad_v], axis=2).reshape(
-        length, 3 * local_heads * HEAD_DIM
-    )
-    qkv_bias_part = jnp.sum(packed_grad, axis=0)
-    packed_bf = packed_grad.astype(jnp.bfloat16)
-    qkv_grad = cross_rows(features, packed_bf)
-    feature_grad = feature_grad + cross_cols(packed_bf, back_qkv)
-    qkv_grad, out_grad, up_grad, down_grad = (
-        lax.psum_scatter(qkv_grad, "fsdp", scatter_dimension=0, tiled=True),
-        lax.psum_scatter(out_grad, "fsdp", scatter_dimension=1, tiled=True),
-        lax.psum_scatter(up_grad, "fsdp", scatter_dimension=0, tiled=True),
-        lax.psum_scatter(down_grad, "fsdp", scatter_dimension=1, tiled=True),
-    )
-    row_grad = lax.psum_scatter(feature_grad, "tp", scatter_dimension=0, tiled=True)
     cot_rows = out_cotangent.astype(jnp.float32)
-    gain_grad, shift_grad, bias_grad = lax.psum(
-        (jnp.sum(row_grad * normed, axis=0), jnp.sum(row_grad, axis=0), jnp.sum(cot_rows, axis=0)),
-        ("fsdp", "tp"),
-    )
-    qkv_bias_grad, up_bias_grad = lax.psum((qkv_bias_part, up_bias_part), "fsdp")
+    model = own_rows.shape[1]
+    biases = jnp.concatenate([qkv_bias_part, up_bias_part])
+    bias_rows = -(-biases.shape[0] // model)
+    biases = jnp.pad(biases, (0, bias_rows * model - biases.shape[0])).reshape(bias_rows, model)
+    pad_rows = jnp.zeros((8 - 3, model), jnp.float32)
+    rows = jnp.concatenate(
+        [
+            jnp.sum(row_grad * normed, axis=0)[None],
+            jnp.sum(row_grad, axis=0)[None],
+            jnp.sum(cot_rows, axis=0)[None],
+            pad_rows,
+            biases,
+            jnp.zeros((-bias_rows % 8, model), jnp.float32),
+        ]
+    )
+    sums = sum_vectors(rows, 8)
+    gain_grad, shift_grad, bias_grad = sums[0], sums[1], sums[2]
+    bias_flat = sums[8 : 8 + bias_rows].reshape(-1)
+    qkv_bias_grad = bias_flat[:width_qkv]
+    up_bias_grad = bias_flat[width_qkv : width_qkv + width_up]
     scaled = row_grad * norm_gain
     input_grad = (
         cot_rows
@@ -255,18 +386,20 @@
             - normed * jnp.mean(scaled * normed, axis=-1, keepdims=True)
         )
     ).astype(jnp.bfloat16)
+    mlp_sum = mlp_sum.astype(jnp.float32)
+    att_sum = att_sum.astype(jnp.float32)
     return (
         layer_output,
         input_grad,
         gain_grad,
         shift_grad,
-        qkv_grad,
+        att_sum[:, :width_qkv],
         qkv_bias_grad,
-        out_grad,
+        att_sum[:, width_qkv:].T,
         bias_grad,
-        up_grad,
+        mlp_sum[:, :width_up],
         up_bias_grad,
-        down_grad,
+        mlp_sum[:, width_up:].T,
         bias_grad,
     )
 

time: 531 us -> 429 us (0.81)
  blocking collectives: 128 us -> 0 us
  matrix products: 89.1 us -> 57.1 us
  local copies, waits for them, and re-layouts: 14.2 us -> 36.5 us
  Pallas kernels: 0 us -> 19.2 us
  waiting for transfers between devices: 258 us -> 271 us
    reduce_scatter x5 -> x2, waiting for transfers between devices: 251 us -> 56 us  [scatter_rows(): lax.psum_scatter(partial.astype(jnp.bfloat16), 'tp', scatter_dimension=0,...]
    unnamed x11 -> x10, waiting for transfers between devices: 7.07 us -> 96.6 us
    all_gather x2, waiting for transfers between devices: 0.02 us -> 87.2 us  [gather_weights(): return lax.all_gather(shard, 'fsdp', axis=0, tiled=True)]
    all_gather x2 -> x0, blocking collectives: 65.9 us -> none  [the longest x1 34.6 us: body(): lax.all_gather(qkv_weight, 'fsdp', axis=0, tiled=True)]
    psum x2 -> x0, blocking collectives: 62.3 us -> none  [the longest x1 40.2 us: body(): lax.psum((jnp.sum(row_grad * normed, axis=0), jnp.sum(row_grad, axis=0),...]
    pallas_call x0 -> x1, Pallas kernels: none -> 19.2 us  [sum_vectors(): pl.pallas_call(functools.partial(vector_sums, fsdp, tp, all_rows), out_sh...]
    all_gather x1, waiting for transfers between devices: 0.02 us -> 17.3 us  [body(): lax.all_gather(shifted.astype(jnp.bfloat16), 'tp', axis=0, tiled=True)]
    dot_general x15 -> x16, matrix products: 26.8 us -> 12.2 us  [cross_rows(): lax.dot_general(left, right, (((0,), (0,)), ((), ())), preferred_element_...]
  transfers between devices with their start and end apart: 10 -> 8, of which waited for: 6 -> 8; matrix products, arithmetic and copies ran while one was open for 23% -> 11% of each run, Pallas kernels for 0% -> 4%
where the time goes in v1:
time: 429 us; the launch traced here: 428 us
  waiting for transfers between devices  271 us (63%)
  matrix products  57.1 us (13%)
  local copies, waits for them, and re-layouts  36.5 us (9%)
  other arithmetic  28.9 us (7%)
  Pallas kernels  19.2 us (4%)
  between operations  14.7 us (3%)
    unnamed x10, waiting for transfers between devices  96.6 us
    all_gather x2, waiting for transfers between devices, gather_weights(): return lax.all_gather(shard, 'fsdp', axis=0, tiled=True)  87.2 us
    reduce_scatter x2, waiting for transfers between devices, scatter_rows(): lax.psum_scatter(partial.astype(jnp.bfloat16), 'tp', scatter_dimension=0,...  56 us
    dot_general x22, matrix products, cross_cols(): lax.dot_general(left, right, (((1,), (1,)), ((), ())), preferred_element_...  23.6 us
    pallas_call x1, Pallas kernels, sum_vectors(): pl.pallas_call(functools.partial(vector_sums, fsdp, tp, all_rows), out_sh...  19.2 us
    all_gather x1, waiting for transfers between devices, body(): lax.all_gather(shifted.astype(jnp.bfloat16), 'tp', axis=0, tiled=True)  17.3 us
    all_gather x1, waiting for transfers between devices, body(): grad_rows = lax.all_gather(out_cotangent, 'tp', axis=0, tiled=True)  13.9 us
    unnamed x74, local copies, waits for them, and re-layouts  13.4 us
  transfers between devices with their start and end apart: 8, of which 8 were waited for; matrix products, arithmetic and copies ran while one was open for 11% of the time, Pallas kernels for 4%

profile of v1, /device:TPU:0, one launch (start us, length us, event | category | flops | bytes accessed | tf_op | source)
XLA Modules:
  0.0 428.1 jit_solution(16750896217507794072)
XLA Ops:
  9.7 2.0 fusion.76
  11.8 1.7 pad_maximum_fusion.3
  17.0 17.3 %all-gather.5.cloned.1.call-done = bf16[1024,768]{1,0:T(8,128)(2,1)} async-done(((bf16[256,768]{1,0:T(8,128)(2,1)}), bf16[1024,768]{1,0:T(8,128)(2,1)}) %all-gather.5.cloned.1.call-update) | async-done | bytes 1572880 | tf_op jit(solution)/shard_map/all_gather | solution.py:317
  34.2 54.6 %all-gather.9.cloned.1.call-done = bf16[768,1536]{1,0:T(8,128)(2,1)} async-done(((bf16[96,1536]{1,0:T(8,128)(2,1)}), bf16[768,1536]{1,0:T(8,128)(2,1)}) %all-gather.9.cloned.1.call-update) | async-done | bytes 2359312 | tf_op jit(solution)/shard_map/all_gather | solution.py:243
  88.9 5.9 %multiply_convert_fusion.1 = (bf16[1024,768]{0,1:T(8,128)(2,1)}, f32[1024,768]{0,1:T(8,128)}) fusion(f32[768]{0:T(1024)S(1)} %copy-done.31, bf16[1024,768]{1,0:T(8,128)(2,1)} %all-gather.5.cloned.1.call-done, bf16[768,1536]{1,0:T(8,128)(2,1)} %all-gather.9.cloned.1.call-done), kind=kOutput, calls=%fused_computation.95 | convolution fusion | flops 1212678144 | bytes 7474176 | tf_op jit(solution)/shard_map/dot_general | solution.py:324
  94.8 13.9 %all-gather.7.cloned.1.call-done = bf16[1024,768]{1,0:T(8,128)(2,1)} async-done(((bf16[256,768]{1,0:T(8,128)(2,1)}), bf16[1024,768]{1,0:T(8,128)(2,1)}) %all-gather.7.cloned.1.call-update) | async-done | bytes 1572880 | tf_op jit(solution)/shard_map/all_gather | solution.py:319
  108.6 5.7 %fusion.99 = (f32[768]{0:T(1024)}, bf16[1024,768]{0,1:T(8,128)(2,1)S(1)}) fusion(f32[1024,768]{0,1:T(8,128)} %get-tuple-element.494, f32[768]{0:T(1024)S(1)} %copy-done.31, bf16[1024,768]{1,0:T(8,128)(2,1)} %all-gather.7.cloned.1.call-done, bf16[768,1536]{1,0:T(8,128)(2,1)S(1)} %copy-done.27), kind=kOutput, calls=%fused_computation.202 | convolution fusion | flops 1217395968 | bytes 7478272 | tf_op jit(solution)/shard_map/dot_general | solution.py:326
  114.4 1.4 convolution_convert_fusion.2
  116.8 1.4 fusion.57
  118.2 1.6 pad_maximum_fusion
  119.8 32.6 %all-gather.11.cloned.1.call-done = bf16[768,768]{1,0:T(8,128)(2,1)} async-done(((bf16[96,768]{1,0:T(8,128)(2,1)}), bf16[768,768]{1,0:T(8,128)(2,1)}) %all-gather.11.cloned.1.call-update) | async-done | bytes 1179664 | tf_op jit(solution)/shard_map/all_gather | solution.py:243
  152.4 2.3 convolution_add_fusion.2
  157.9 2.5 convolution_convert_fusion.5
  161.8 1.4 copy.104
  163.2 1.8 fusion.90
  166.4 1.7 maximum_bitcast_fusion.6
  169.4 10.0 %while.28 = (s32[]{:T(128)}, bf16[3,1024,64]{1,2,0:T(8,128)(2,1)S(1)}, f32[3,1024,1]{1,2,0:T(1,128)}, s32[1024]{0:T(1024)S(1)}, bf16[3,1024,64]{2,1,0:T(8,128)(2...) while((s32[]{:T(128)}, ...), condition=%wide.region_9.10_spmd, body=%wide.region_4.9_spmd.sunk | while | flops 209518592 | bytes 10947217 | solution.py:273
  179.4 30.5 %while.29 = (s32[]{:T(128)}, f32[3,1024,64]{1,2,0:T(8,128)}, f32[3,1024,64]{1,2,0:T(8,128)}, f32[3,1024,64]{1,2,0:T(8,128)}, s32[1024]{0:T(1024)S(1)}, /*index=5...) while((s32[]{:T(128)}, f32[3,1024,64]{1,2,0:T(8,128)}, ...), condition=%wide.region_13.14_spmd, body=%wide.region_11.13_spmd.sunk | while | flops 512424960 | bytes 22216956 | solution.py:285
  216.9 1.5 copy.116
  218.5 3.3 fusion.62
  221.8 2.6 add_convert_fusion
  224.5 3.2 fusion.66
  227.7 3.1 add_convert_fusion.1
  230.9 2.7 copy.118
  235.4 46.8 %reduce-scatter.13.cloned.1.call-done = bf16[96,768]{1,0:T(8,128)(2,1)} async-done(((bf16[768,768]{1,0:T(8,128)(2,1)}), bf16[96,768]{1,0:T(8,128)(2,1)}) %reduce-scatter.13.cloned.1.call-update) | async-done | bytes 147472
  284.8 26.9 %reduce-scatter.11.cloned.1.call-done = bf16[256,768]{1,0:T(8,128)(2,1)} async-done(((bf16[1024,768]{1,0:T(8,128)(2,1)}), bf16[256,768]{1,0:T(8,128)(2,1)}) %reduce-scatter.11.cloned.1.call-update) | async-done | bytes 393232 | tf_op jit(solution)/shard_map/reduce_scatter | solution.py:253
  311.6 1.4 fusion.85
  313.1 29.1 %reduce-scatter.9.cloned.1.call-done = bf16[256,768]{1,0:T(8,128)(2,1)} async-done(((bf16[1024,768]{1,0:T(8,128)(2,1)}), bf16[256,768]{1,0:T(8,128)(2,1)}) %reduce-scatter.9.cloned.1.call-update) | async-done | bytes 393232 | tf_op jit(solution)/shard_map/reduce_scatter | solution.py:253
  342.2 2.4 convert_reduce_fusion.2
  345.9 19.2 %vector_sums.1 = f32[16,768]{1,0:T(8,128)} custom-call(f32[16,768]{1,0:T(8,128)} %concatenate.83.rows_ref), custom_call_target="tpu_custom_call" | custom-call | tf_op jit(solution)/shard_map/vector_sums/pallas_call | solution.py:224
  367.1 1.5 slice_reduce_fusion.1
  368.6 49.0 %reduce-scatter.15.cloned.1.call-done = bf16[96,1536]{1,0:T(8,128)(2,1)} async-done(((bf16[768,1536]{1,0:T(8,128)(2,1)}), bf16[96,1536]{1,0:T(8,128)(2,1)}) %reduce-scatter.15.cloned.1.call-update) | async-done | bytes 294928
  (262 shorter events, 72.4 us)
Async XLA Ops:
  7.2 7.1 %copy-start.17 = (bf16[192,96]{1,0:T(8,128)(2,1)S(1)}, bf16[192,96]{1,0:T(8,128)(2,1)}, u32[]{:S(2)}) copy-start(bf16[192,96]{1,0:T(8,128)(2,1)} %param.24) | copy-start | bytes 110596
  7.2 7.2 %copy-start.16 = (bf16[96,576]{1,0:T(8,128)(2,1)S(1)}, bf16[96,576]{1,0:T(8,128)(2,1)}, u32[]{:S(2)}) copy-start(bf16[96,576]{1,0:T(8,128)(2,1)} %param.22) | copy-start | bytes 331780
  7.2 8.1 %copy-start.14 = (s32[1,1024]{1,0:T(1,128)S(1)}, s32[1,1024]{1,0:T(1,128)}, u32[]{:S(2)}) copy-start(s32[1,1024]{1,0:T(1,128)} %param.19) | copy-start | bytes 12292
  7.2 81.7 %copy-start.31 = (f32[768]{0:T(1024)S(1)}, f32[768]{0:T(1024)}, u32[]{:S(2)}) copy-start(f32[768]{0:T(1024)} %param.27) | copy-start | bytes 9220
  7.2 27.0 %all-gather.5.cloned.1.call-start = ((), (), s32[]{:S(2)}) async-start(), calls=%async_computation.4 | async-start | bytes 1966080 | tf_op jit(solution)/shard_map/all_gather | solution.py:317
  8.4 6.9 %copy-start.19 = (f32[256]{0:T(256)}, f32[256]{0:T(256)S(1)}, u32[]{:S(2)}) copy-start(f32[256]{0:T(256)S(1)} %broadcast_multiply_fusion.2) | copy-start | bytes 3076
  9.7 5.6 %copy-start.21 = (f32[256]{0:T(256)}, f32[256]{0:T(256)S(1)}, u32[]{:S(2)}) copy-start(f32[256]{0:T(256)S(1)} %add_rsqrt_fusion) | copy-start | bytes 3076
  11.7 77.1 %all-gather.9.cloned.1.call-start = ((), (), s32[]{:S(2)}) async-start(), calls=%async_computation.6 | async-start | bytes 2654208 | tf_op jit(solution)/shard_map/all_gather | solution.py:243
  13.5 95.1 %all-gather.7.cloned.1.call-start = ((), (), s32[]{:S(2)}) async-start(), calls=%async_computation.5 | async-start | bytes 1966080 | tf_op jit(solution)/shard_map/all_gather | solution.py:319
  14.3 138.1 %all-gather.11.cloned.1.call-start = ((), (), s32[]{:S(2)}) async-start(), calls=%async_computation.7 | async-start | bytes 1327104 | tf_op jit(solution)/shard_map/all_gather | solution.py:243
  15.2 266.9 %reduce-scatter.13.cloned.1.call-start = ((), (), s32[]{:S(2)}) async-start(), calls=%async_computation.10 | async-start | bytes 1327104
  88.9 19.8 %copy-start.27 = (bf16[768,1536]{1,0:T(8,128)(2,1)S(1)}, bf16[768,1536]{1,0:T(8,128)(2,1)}, u32[]{:S(2)}) copy-start(bf16[768,1536]{1,0:T(8,128)(2,1)} %all-gather.9.cloned.1.call-done) | copy-start | bytes 7077892
  108.6 5.7 %copy-start.28 = (bf16[1024,768]{1,0:T(8,128)(2,1)S(1)}, bf16[1024,768]{1,0:T(8,128)(2,1)}, u32[]{:S(2)}) copy-start(bf16[1024,768]{1,0:T(8,128)(2,1)} %all-gather.5.cloned.1.call-done) | copy-start | bytes 4718596
  114.4 2.4 copy-start.33
  118.2 34.2 %copy-start.29 = (bf16[1024,768]{1,0:T(8,128)(2,1)S(1)}, bf16[1024,768]{1,0:T(8,128)(2,1)}, u32[]{:S(2)}) copy-start(bf16[1024,768]{1,0:T(8,128)(2,1)} %all-gather.5.cloned.1.call-done) | copy-start | bytes 4718596
  118.2 34.2 %copy-start.32 = (f32[576]{0:T(1024)S(1)}, f32[576]{0:T(1024)}, u32[]{:S(2)}) copy-start(f32[576]{0:T(1024)} %param.23) | copy-start | bytes 6916
  197.5 2.3 copy-start.7
  209.9 2.3 copy-start.11
  209.9 2.4 copy-start.13
  218.4 3.4 copy-start.15
  218.4 93.2 %reduce-scatter.11.cloned.1.call-start = ((), (), s32[]{:S(2)}) async-start(), calls=%async_computation.9 | async-start | bytes 1966080 | tf_op jit(solution)/shard_map/reduce_scatter | solution.py:253
  224.4 117.8 %reduce-scatter.9.cloned.1.call-start = ((), (), s32[]{:S(2)}) async-start(), calls=%async_computation.8 | async-start | bytes 1966080 | tf_op jit(solution)/shard_map/reduce_scatter | solution.py:253
  227.7 3.2 copy-start.1
  230.8 186.8 %reduce-scatter.15.cloned.1.call-start = ((), (), s32[]{:S(2)}) async-start(), calls=%async_computation.11 | async-start | bytes 2654208
  234.9 76.7 %copy-start = (bf16[256,768]{1,0:T(8,128)(2,1)S(1)}, bf16[256,768]{1,0:T(8,128)(2,1)}, u32[]{:S(2)}) copy-start(bf16[256,768]{1,0:T(8,128)(2,1)} %param.17) | copy-start | bytes 1179652
  234.9 76.7 %copy-start.18 = (f32[768]{0:T(1024)S(1)}, f32[768]{0:T(1024)}, u32[]{:S(2)}) copy-start(f32[768]{0:T(1024)} %param.20) | copy-start | bytes 9220
  234.9 76.7 %copy-start.20 = (f32[256]{0:T(256)S(1)}, f32[256]{0:T(256)}, u32[]{:S(2)}) copy-start(f32[256]{0:T(256)} %copy-done.19) | copy-start | bytes 3076
  235.0 76.7 %copy-start.22 = (f32[256]{0:T(256)S(1)}, f32[256]{0:T(256)}, u32[]{:S(2)}) copy-start(f32[256]{0:T(256)} %copy-done.21) | copy-start | bytes 3076
  235.1 107.1 %copy-start.10 = (bf16[256,768]{1,0:T(8,128)(2,1)S(1)}, bf16[256,768]{1,0:T(8,128)(2,1)}, u32[]{:S(2)}) copy-start(bf16[256,768]{1,0:T(8,128)(2,1)} %param.18) | copy-start | bytes 1179652
  235.2 107.1 %copy-start.24 = (f32[768]{0:T(1024)S(1)}, f32[768]{0:T(1024)}, u32[]{:S(2)}) copy-start(f32[768]{0:T(1024)} %param.29) | copy-start | bytes 9220
  235.2 107.1 %copy-start.25 = (f32[768]{0:T(1024)S(1)}, f32[768]{0:T(1024)}, u32[]{:S(2)}) copy-start(f32[768]{0:T(1024)} %param.25) | copy-start | bytes 9220
  368.6 52.1 %copy-start.23 = (f32[768]{0:T(1024)}, f32[768]{0:T(1024)S(1)}, u32[]{:S(2)}) copy-start(f32[768]{0:T(1024)S(1)} %get-tuple-element.747) | copy-start | bytes 9220
  (15 other events, 25.0 us)
Sparse Core Ops, SparseCore 0:
  11.9 22.3 all-gather.4
  37.0 51.8 all-gather.8
  90.4 18.1 all-gather.6
  111.2 41.1 all-gather.10
  218.5 63.5 reduce-scatter.12
  284.5 27.0 reduce-scatter.10
  314.1 28.0 reduce-scatter.8
  345.7 71.8 reduce-scatter.14

commit v2 on v1

--- a/solution.py
+++ b/solution.py
@@ -150,109 +150,335 @@
 MESH = pl.DeviceIdType.MESH
 
 
-def vector_sums(fsdp, tp, all_rows, rows_ref, out_ref, first, second, send, recv, send2, recv2):
+def place(fsdp, tp):
     f = lax.axis_index("fsdp")
     t = lax.axis_index("tp")
+    pair = lax.rem(f, 2)
+    line = lax.div(f, 2)
+    return f, t, pair, line
+
+
+def remote(source, target, send, recv, device):
+    return pltpu.make_async_remote_copy(
+        src_ref=source,
+        dst_ref=target,
+        send_sem=send,
+        recv_sem=recv,
+        device_id=device,
+        device_id_type=MESH,
+    )
+
+
+def each(first, last, action):
+    def step_of(step, carry):
+        action(step)
+        return carry
+
+    lax.fori_loop(first, last, step_of, 0)
+
+
+def greet(fsdp, tp):
+    f, t, _, _ = place(fsdp, tp)
     barrier = pltpu.get_barrier_semaphore()
-
-    def greet_f(step, carry):
-        pl.semaphore_signal(
+    each(
+        1,
+        fsdp,
+        lambda step: pl.semaphore_signal(
             barrier, inc=1, device_id=(lax.rem(f + step, fsdp), t), device_id_type=MESH
-        )
-        return carry
-
-    def greet_t(step, carry):
-        pl.semaphore_signal(
+        ),
+    )
+    each(
+        1,
+        tp,
+        lambda step: pl.semaphore_signal(
             barrier, inc=1, device_id=(f, lax.rem(t + step, tp)), device_id_type=MESH
-        )
-        return carry
-
-    lax.fori_loop(1, fsdp, greet_f, 0)
-    lax.fori_loop(1, tp, greet_t, 0)
+        ),
+    )
     pl.semaphore_wait(barrier, fsdp + tp - 2)
 
-    def copy_f(step, source):
-        return pltpu.make_async_remote_copy(
-            src_ref=rows_ref,
-            dst_ref=first.at[source],
-            send_sem=send.at[step],
-            recv_sem=recv.at[step],
-            device_id=(lax.rem(f + step, fsdp), t),
-            device_id_type=MESH,
-        )
-
-    def start_f(step, carry):
-        copy_f(step, f).start()
-        return carry
-
-    def wait_f(step, carry):
-        copy_f(step, lax.rem(f + fsdp - step, fsdp)).wait()
-        return carry
-
-    lax.fori_loop(1, fsdp, start_f, 0)
-    first[f] = rows_ref[...]
-    lax.fori_loop(1, fsdp, wait_f, 0)
-    total = lax.fori_loop(
-        1, fsdp, lambda step, value: value + first[step], first[0]
-    )
-    second[t] = total[:all_rows]
-
-    def copy_t(step, source):
-        return pltpu.make_async_remote_copy(
-            src_ref=second.at[t],
-            dst_ref=second.at[source],
-            send_sem=send2.at[step],
-            recv_sem=recv2.at[step],
-            device_id=(f, lax.rem(t + step, tp)),
-            device_id_type=MESH,
-        )
-
-    for step in range(1, tp):
-        copy_t(step, t).start()
-    for step in range(1, tp):
-        copy_t(step, lax.rem(t + tp - step, tp)).wait()
+
+def gather_kernel(
+    fsdp, tp, w_ref, h_ref, c_ref, w_out, h_out, c_out, w_send, w_recv, p_send, p_recv, r_send, r_recv
+):
+    f, t, pair, line = place(fsdp, tp)
+    lines = fsdp // 2
+    greet(fsdp, tp)
+    partner = 2 * line + 1 - pair
+
+    def along(step, slot):
+        other = lax.rem(line + step, lines)
+        return remote(
+            w_ref, w_out.at[slot], w_send.at[step], w_recv.at[step], (2 * other + pair, t)
+        )
+
+    def across(step, source, slot):
+        return remote(source, w_out.at[slot], p_send.at[step], p_recv.at[step], (partner, t))
+
+    def beside(step, which, source, target, slot):
+        return remote(
+            source,
+            target.at[slot],
+            r_send.at[which, step],
+            r_recv.at[which, step],
+            (f, lax.rem(t + step, tp)),
+        )
+
+    def came(step, side):
+        return 2 * lax.rem(line + lines - step, lines) + side
+
+    across(0, w_ref, f).start()
+    each(1, lines, lambda step: along(step, f).start())
+    each(1, tp, lambda step: beside(step, 0, h_ref, h_out, t).start())
+    each(1, tp, lambda step: beside(step, 1, c_ref, c_out, t).start())
+    w_out[f] = w_ref[...]
+    h_out[t] = h_ref[...]
+    c_out[t] = c_ref[...]
+
+    def forward(step):
+        slot = came(step, pair)
+        along(step, slot).wait_recv()
+        across(step, w_out.at[slot], slot).start()
+
+    each(1, lines, forward)
+
+    def settle(step):
+        slot = lax.rem(t + tp - step, tp)
+        beside(step, 0, h_ref, h_out, slot).wait()
+        beside(step, 1, c_ref, c_out, slot).wait()
+
+    each(1, tp, settle)
+    each(1, lines, lambda step: along(step, f).wait_send())
+
+    def finish(step):
+        across(step, w_ref, came(step, 1 - pair)).wait()
+
+    each(0, lines, finish)
+
+
+def gather_all(weights, features, cotangent):
+    fsdp = lax.axis_size("fsdp")
+    tp = lax.axis_size("tp")
+    vmem = pl.BlockSpec(memory_space=pltpu.VMEM)
+    shapes = (
+        jax.ShapeDtypeStruct((fsdp,) + weights.shape, weights.dtype),
+        jax.ShapeDtypeStruct((tp,) + features.shape, features.dtype),
+        jax.ShapeDtypeStruct((tp,) + cotangent.shape, cotangent.dtype),
+    )
+    dma = pltpu.SemaphoreType.DMA
+    w_all, h_all, c_all = pl.pallas_call(
+        functools.partial(gather_kernel, fsdp, tp),
+        out_shape=shapes,
+        in_specs=[vmem] * 3,
+        out_specs=(vmem,) * 3,
+        scratch_shapes=[
+            dma((fsdp // 2,)),
+            dma((fsdp // 2,)),
+            dma((fsdp // 2,)),
+            dma((fsdp // 2,)),
+            dma((2, tp)),
+            dma((2, tp)),
+        ],
+        compiler_params=pltpu.CompilerParams(
+            collective_id=1, has_side_effects=True, vmem_limit_bytes=48 * 1024 * 1024
+        ),
+        name="gather_all",
+    )(weights, features, cotangent)
+    return (
+        w_all.reshape(fsdp * weights.shape[0], weights.shape[1]),
+        h_all.reshape(tp * features.shape[0], features.shape[1]),
+        c_all.reshape(tp * cotangent.shape[0], cotangent.shape[1]),
+    )
+
+
+def scatter_kernel(
+    fsdp,
+    tp,
+    g_ref,
+    b_ref,
+    d_ref,
+    n_ref,
+    v_ref,
+    g_out,
+    b_out,
+    d_out,
+    v_out,
+    halves,
+    joined,
+    lands,
+    b_land,
+    d_land,
+    rows,
+    first,
+    second,
+    p_send,
+    p_recv,
+    w_send,
+    w_recv,
+    r_send,
+    r_recv,
+    v_send,
+    v_recv,
+    u_send,
+    u_recv,
+):
+    f, t, pair, line = place(fsdp, tp)
+    lines = fsdp // 2
+    greet(fsdp, tp)
+    partner = 2 * line + 1 - pair
+
+    def ahead(step):
+        return lax.rem(line + step, lines)
+
+    def across(step):
+        return remote(
+            g_ref.at[2 * ahead(step) + 1 - pair],
+            halves.at[step],
+            p_send.at[step],
+            p_recv.at[step],
+            (partner, t),
+        )
+
+    def along(step):
+        return remote(
+            joined.at[step],
+            lands.at[step],
+            w_send.at[step],
+            w_recv.at[step],
+            (2 * ahead(step) + pair, t),
+        )
+
+    def beside(step, which, source, target):
+        return remote(
+            source.at[lax.rem(t + step, tp)],
+            target.at[step],
+            r_send.at[which, step],
+            r_recv.at[which, step],
+            (f, lax.rem(t + step, tp)),
+        )
+
+    def start_beside(step):
+        beside(step, 1, d_ref, d_land).start()
+        beside(step, 0, b_ref, b_land).start()
+
+    each(1, lines, lambda step: across(step).start())
+    across(0).start()
+    each(1, tp, start_beside)
+
+    def join(step):
+        across(step).wait_recv()
+        joined[step] = (
+            g_ref[2 * ahead(step) + pair].astype(jnp.float32)
+            + halves[step].astype(jnp.float32)
+        ).astype(joined.dtype)
+        along(step).start()
+
+    each(1, lines, join)
+    across(0).wait_recv()
+    g_out[...] = g_ref[f].astype(jnp.float32) + halves[0].astype(jnp.float32)
+
+    d_out[...] = d_ref[t].astype(jnp.float32)
+    b_out[...] = b_ref[t].astype(jnp.float32)
+
+    def gather_d(step):
+        beside(step, 1, d_ref, d_land).wait()
+        d_out[...] += d_land[step].astype(jnp.float32)
+
+    def gather_b(step):
+        beside(step, 0, b_ref, b_land).wait()
+        b_out[...] += b_land[step].astype(jnp.float32)
+
+    each(1, tp, gather_d)
+    rows[...] = v_ref[...]
+    rows[0:1] = jnp.sum(d_out[...] * n_ref[...], axis=0, keepdims=True)
+    rows[1:2] = jnp.sum(d_out[...], axis=0, keepdims=True)
+
+    def spread(step, slot):
+        return remote(
+            rows,
+            first.at[slot],
+            v_send.at[step],
+            v_recv.at[step],
+            (lax.rem(f + step, fsdp), t),
+        )
+
+    each(1, fsdp, lambda step: spread(step, f).start())
+    first[f] = rows[...]
+    each(1, tp, gather_b)
+
+    def collect(step):
+        along(step).wait_recv()
+        g_out[...] += lands[step].astype(jnp.float32)
+
+    each(1, lines, collect)
+    each(1, fsdp, lambda step: spread(step, lax.rem(f + fsdp - step, fsdp)).wait())
+    total = lax.fori_loop(1, fsdp, lambda step, value: value + first[step], first[0])
+    second[t] = total[:8]
+    v_out[...] = total
+
+    def share(step, slot):
+        return remote(
+            second.at[t],
+            second.at[slot],
+            u_send.at[step],
+            u_recv.at[step],
+            (f, lax.rem(t + step, tp)),
+        )
+
+    each(1, tp, lambda step: share(step, t).start())
+    each(1, lines, lambda step: along(step).wait_send())
+    each(0, lines, lambda step: across(step).wait_send())
+    each(1, tp, lambda step: share(step, lax.rem(t + tp - step, tp)).wait())
     whole = second[0]
     for step in range(1, tp):
         whole = whole + second[step]
-    out_ref[:all_rows] = whole
-    out_ref[all_rows:] = total[all_rows:]
-
-
-def sum_vectors(rows, all_rows):
+    v_out[:8] = whole
+
+
+def scatter_all(grads, branch, feature_grad, normed, vectors):
     fsdp = lax.axis_size("fsdp")
     tp = lax.axis_size("tp")
+    lines = fsdp // 2
+    grads = grads.reshape(fsdp, -1, grads.shape[1])
+    branch = branch.reshape(tp, -1, branch.shape[1])
+    feature_grad = feature_grad.reshape(tp, -1, feature_grad.shape[1])
+    vmem = pl.BlockSpec(memory_space=pltpu.VMEM)
+    dma = pltpu.SemaphoreType.DMA
+    f32 = jnp.float32
     return pl.pallas_call(
-        functools.partial(vector_sums, fsdp, tp, all_rows),
-        out_shape=jax.ShapeDtypeStruct(rows.shape, jnp.float32),
-        in_specs=[pl.BlockSpec(memory_space=pltpu.VMEM)],
-        out_specs=pl.BlockSpec(memory_space=pltpu.VMEM),
+        functools.partial(scatter_kernel, fsdp, tp),
+        out_shape=(
+            jax.ShapeDtypeStruct(grads.shape[1:], f32),
+            jax.ShapeDtypeStruct(branch.shape[1:], f32),
+            jax.ShapeDtypeStruct(feature_grad.shape[1:], f32),
+            jax.ShapeDtypeStruct(vectors.shape, f32),
+        ),
+        in_specs=[vmem] * 5,
+        out_specs=(vmem,) * 4,
         scratch_shapes=[
-            pltpu.VMEM((fsdp,) + rows.shape, jnp.float32),
-            pltpu.VMEM((tp, all_rows, rows.shape[1]), jnp.float32),
-            pltpu.SemaphoreType.DMA((fsdp,)),
-            pltpu.SemaphoreType.DMA((fsdp,)),
-            pltpu.SemaphoreType.DMA((tp,)),
-            pltpu.SemaphoreType.DMA((tp,)),
+            pltpu.VMEM((lines,) + grads.shape[1:], grads.dtype),
+            pltpu.VMEM((lines,) + grads.shape[1:], grads.dtype),
+            pltpu.VMEM((lines,) + grads.shape[1:], grads.dtype),
+            pltpu.VMEM(branch.shape, branch.dtype),
+            pltpu.VMEM(feature_grad.shape, feature_grad.dtype),
+            pltpu.VMEM(vectors.shape, f32),
+            pltpu.VMEM((fsdp,) + vectors.shape, f32),
+            pltpu.VMEM((tp, 8, vectors.shape[1]), f32),
+            dma((lines,)),
+            dma((lines,)),
+            dma((lines,)),
+            dma((lines,)),
+            dma((2, tp)),
+            dma((2, tp)),
+            dma((fsdp,)),
+            dma((fsdp,)),
+            dma((tp,)),
+            dma((tp,)),
         ],
-        compiler_params=pltpu.CompilerParams(collective_id=1, has_side_effects=True),
-        name="vector_sums",
-    )(rows)
-
-
-def gather_weights(shard):
-    return lax.all_gather(shard, "fsdp", axis=0, tiled=True)
-
-
-def scatter_grads(grads):
-    return lax.psum_scatter(
-        grads.astype(jnp.bfloat16), "fsdp", scatter_dimension=0, tiled=True
-    )
-
-
-def scatter_rows(partial):
-    return lax.psum_scatter(
-        partial.astype(jnp.bfloat16), "tp", scatter_dimension=0, tiled=True
-    ).astype(jnp.float32)
+        compiler_params=pltpu.CompilerParams(
+            collective_id=2, has_side_effects=True, vmem_limit_bytes=56 * 1024 * 1024
+        ),
+        name="scatter_all",
+    )(grads, branch, feature_grad, normed, vectors)
 
 
 def attention_branch(features, grad_rows, qkv_full, qkv_bias, out_full, segment_row):
@@ -314,12 +540,13 @@
     width_up = up_weight.shape[1]
     own_rows = layer_input.astype(jnp.float32)
     normed, inverse, shifted = layer_norm(own_rows, norm_gain, norm_bias)
-    features = lax.all_gather(shifted.astype(jnp.bfloat16), "tp", axis=0, tiled=True)
-    mlp_full = gather_weights(jnp.concatenate([up_weight, down_weight.T], axis=1))
-    grad_rows = lax.all_gather(out_cotangent, "tp", axis=0, tiled=True)
-    att_full = gather_weights(jnp.concatenate([qkv_weight, out_weight.T], axis=1))
-    full_up, full_down = mlp_full[:, :width_up], mlp_full[:, width_up:]
-    full_qkv, full_out = att_full[:, :width_qkv], att_full[:, width_qkv:]
+    w_all, features, grad_rows = gather_all(
+        jnp.concatenate([up_weight, down_weight.T, qkv_weight, out_weight.T], axis=1),
+        shifted.astype(jnp.bfloat16),
+        out_cotangent,
+    )
+    ends = (width_up, 2 * width_up, 2 * width_up + width_qkv)
+    full_up, full_down, full_qkv, full_out = jnp.split(w_all, ends, axis=1)
 
     pre_act = jnp.dot(features, full_up, preferred_element_type=jnp.float32) + up_bias
     gelu_rows = gelu_value(pre_act).astype(jnp.bfloat16)
@@ -328,50 +555,42 @@
     )
     pre_grads = grad_pre.astype(jnp.bfloat16)
     up_bias_part = jnp.sum(grad_pre, axis=0)
-    mlp_grad = jnp.concatenate(
+    mixed_rows, packed_bf, qkv_bias_part = attention_branch(
+        features, grad_rows, full_qkv, qkv_bias, full_out, segments[0]
+    )
+    branch = cross_cols(mixed_rows, full_out) + cross_cols(gelu_rows, full_down)
+    feature_grad = cross_cols(packed_bf, full_qkv) + cross_cols(pre_grads, full_up)
+    grads = jnp.concatenate(
         [
             cross_rows(features, pre_grads).astype(jnp.bfloat16),
             cross_rows(grad_rows, gelu_rows).astype(jnp.bfloat16),
-        ],
-        axis=1,
-    )
-    features_late, grad_late, mlp_grad, pre_grads = lax.optimization_barrier(
-        (features, grad_rows, mlp_grad, pre_grads)
-    )
-    mlp_sum = scatter_grads(mlp_grad)
-    mixed_rows, packed_bf, qkv_bias_part = attention_branch(
-        features_late, grad_late, full_qkv, qkv_bias, full_out, segments[0]
-    )
-    partial_value = cross_cols(mixed_rows, full_out) + cross_cols(gelu_rows, full_down)
-    branch = scatter_rows(partial_value)
-    feature_grad = cross_cols(packed_bf, full_qkv) + cross_cols(pre_grads, full_up)
-    row_grad = scatter_rows(feature_grad)
-    att_grad = jnp.concatenate(
-        [
             cross_rows(features, packed_bf).astype(jnp.bfloat16),
             cross_rows(grad_rows, mixed_rows).astype(jnp.bfloat16),
         ],
         axis=1,
     )
-    att_sum = scatter_grads(att_grad)
-    layer_output = (own_rows + branch + out_bias + down_bias).astype(jnp.bfloat16)
     cot_rows = out_cotangent.astype(jnp.float32)
     model = own_rows.shape[1]
     biases = jnp.concatenate([qkv_bias_part, up_bias_part])
     bias_rows = -(-biases.shape[0] // model)
     biases = jnp.pad(biases, (0, bias_rows * model - biases.shape[0])).reshape(bias_rows, model)
-    pad_rows = jnp.zeros((8 - 3, model), jnp.float32)
-    rows = jnp.concatenate(
+    vectors = jnp.concatenate(
         [
-            jnp.sum(row_grad * normed, axis=0)[None],
-            jnp.sum(row_grad, axis=0)[None],
+            jnp.zeros((2, model), jnp.float32),
             jnp.sum(cot_rows, axis=0)[None],
-            pad_rows,
+            jnp.zeros((5, model), jnp.float32),
             biases,
             jnp.zeros((-bias_rows % 8, model), jnp.float32),
         ]
     )
-    sums = sum_vectors(rows, 8)
+    grad_sum, branch, row_grad, sums = scatter_all(
+        grads,
+        branch.astype(jnp.bfloat16),
+        feature_grad.astype(jnp.bfloat16),
+        normed,
+        vectors,
+    )
+    layer_output = (own_rows + branch + out_bias + down_bias).astype(jnp.bfloat16)
     gain_grad, shift_grad, bias_grad = sums[0], sums[1], sums[2]
     bias_flat = sums[8 : 8 + bias_rows].reshape(-1)
     qkv_bias_grad = bias_flat[:width_qkv]
@@ -386,20 +605,19 @@
             - normed * jnp.mean(scaled * normed, axis=-1, keepdims=True)
         )
     ).astype(jnp.bfloat16)
-    mlp_sum = mlp_sum.astype(jnp.float32)
-    att_sum = att_sum.astype(jnp.float32)
+    up_grad, down_grad, qkv_grad, out_grad = jnp.split(grad_sum, ends, axis=1)
     return (
         layer_output,
         input_grad,
         gain_grad,
         shift_grad,
-        att_sum[:, :width_qkv],
+        qkv_grad,
         qkv_bias_grad,
-        att_sum[:, width_qkv:].T,
+        out_grad.T,
         bias_grad,
-        mlp_sum[:, :width_up],
+        up_grad,
         up_bias_grad,
-        mlp_sum[:, width_up:].T,
+        down_grad.T,
         bias_grad,
     )
 

time: 429 us -> 280 us (0.65)
  waiting for transfers between devices: 271 us -> 0 us
  Pallas kernels: 19.2 us -> 134 us
  between operations: 14.7 us -> 1.18 us
  local copies, waits for them, and re-layouts: 36.5 us -> 49 us
  matrix products: 57.1 us -> 62.4 us
    all_gather x4 -> x0, waiting for transfers between devices: 118 us -> none  [the longest x2 87.2 us: gather_weights(): return lax.all_gather(shard, 'fsdp', axis=0, tiled=True)]
    pallas_call x1 -> x2, Pallas kernels: 19.2 us -> 134 us  [the longest x1 75.5 us: scatter_all(): pl.pallas_call(functools.partial(scatter_kernel, fsdp, tp), out_shape=(ja...]
    unnamed x10 -> x0, waiting for transfers between devices: 96.6 us -> none
    reduce_scatter x2 -> x0, waiting for transfers between devices: 56 us -> none  [scatter_rows(): lax.psum_scatter(partial.astype(jnp.bfloat16), 'tp', scatter_dimension=0,...]
    unnamed x74 -> x81, local copies, waits for them, and re-layouts: 13.4 us -> 5.31 us
    concatenate x1 -> x3, local copies, waits for them, and re-layouts: 1.25 us -> 8.3 us  [the longest x1 5.91 us: body(): jnp.concatenate([cross_rows(features, pre_grads).astype(jnp.bfloat16), cr...]
    dynamic_slice x6, local copies, waits for them, and re-layouts: 3.24 us -> 9.93 us  [attention_branch(): mixed, log_total = lax.map(forward_head, (queries, keys_all, values_all))]
    dot_general x16, matrix products: 12.2 us -> 18.7 us  [cross_rows(): lax.dot_general(left, right, (((0,), (0,)), ((), ())), preferred_element_...]
  transfers between devices with their start and end apart: 8 -> 0, of which waited for: 8 -> 0; matrix products, arithmetic and copies ran while one was open for 11% -> 0% of each run, Pallas kernels for 4% -> 0%
where the time goes in v2:
time: 280 us; the launch traced here: 278 us
  Pallas kernels  134 us (48%)
  matrix products  62.4 us (22%)
  local copies, waits for them, and re-layouts  49 us (18%)
  other arithmetic  31.1 us (11%)
    pallas_call x1, Pallas kernels, scatter_all(): pl.pallas_call(functools.partial(scatter_kernel, fsdp, tp), out_shape=(ja...  75.5 us
    pallas_call x1, Pallas kernels, gather_all(): pl.pallas_call(functools.partial(gather_kernel, fsdp, tp), out_shape=shap...  58 us
    dot_general x22, matrix products, cross_cols(): lax.dot_general(left, right, (((1,), (1,)), ((), ())), preferred_element_...  27.1 us
    dot_general x16, matrix products, cross_rows(): lax.dot_general(left, right, (((0,), (0,)), ((), ())), preferred_element_...  18.7 us
    dynamic_slice x6, local copies, waits for them, and re-layouts, attention_branch(): mixed, log_total = lax.map(forward_head, (queries, keys_all, values_all))  9.93 us
    concatenate x1, local copies, waits for them, and re-layouts, body(): jnp.concatenate([cross_rows(features, pre_grads).astype(jnp.bfloat16), cr...  5.91 us

profile of v2, /device:TPU:0, one launch (start us, length us, event | category | flops | bytes accessed | tf_op | source)
XLA Modules:
  0.0 277.6 jit_solution(12185472927843755986)
XLA Ops:
  10.4 58.0 %gather_all.1 = (bf16[8,96,2304]{2,1,0:T(8,128)(2,1)}, bf16[4,256,768]{2,1,0:T(8,128)(2,1)S(1)}, bf16[4,256,768]{2,1,0:T(8,128)(2,1)S(1)}) custom-call(bf16[96,2304]{1,0:T(8,128)(2,1)S(1)} %concatenate.61.w_ref, bf16[256,768]{1,0:T(8,128)(2,1)S(1)} %get-tuple-element.451.h_ref, bf16[256,768]{1,0:T(8,128)(2,1)S(1)} %copy-done), custom_call_target="tpu_custom_call" | custom-call | tf_op jit(solution)/shard_map/gather_all/pallas_call | solution.py:268
  69.6 2.6 convolution_convert_fusion.5
  72.2 2.2 copy.81
  74.4 2.3 convolution_add_fusion.2
  80.1 2.1 copy.80
  86.1 2.2 copy.82
  88.3 2.2 copy.83
  90.5 18.1 %while.28 = (s32[]{:T(128)}, bf16[3,1024,64]{1,2,0:T(8,128)(2,1)}, f32[3,1024,1]{1,2,0:T(1,128)}, s32[1024]{0:T(1024)S(1)}, bf16[3,1024,64]{2,1,0:T(8,128)(2,1)}...) while((s32[]{:T(128)}, bf16[3,1024,64]{1,2,0:T(8,128)(2,1)}, ...), condition=%wide.region_9.10_spmd, body=%wide.region_4.9_spmd.sunk | while | flops 209518592 | bytes 12520109 | solution.py:499
  92.4 1.7 fusion.139
  98.4 1.7 fusion.139
  104.4 1.7 fusion.139
  108.5 42.6 %while.29 = (s32[]{:T(128)}, f32[3,1024,64]{1,2,0:T(8,128)}, f32[3,1024,64]{1,2,0:T(8,128)}, f32[3,1024,64]{1,2,0:T(8,128)}, s32[1024]{0:T(1024)S(1)}, /*index=5...) while((s32[]{:T(128)}, f32[3,1024,64]{1,2,0:T(8,128)}, ...), condition=%wide.region_12.13_spmd, body=%wide.region_10.12_spmd.sunk | while | flops 512424960 | bytes 25362740 | solution.py:511
  110.4 1.6 constant_dynamic-slice_fusion.6
  111.9 1.7 copy.93
  124.6 1.6 constant_dynamic-slice_fusion.6
  126.1 1.7 copy.93
  138.7 1.6 constant_dynamic-slice_fusion.6
  140.3 1.7 copy.93
  151.2 2.3 convolution_convert_fusion.6
  156.5 3.4 %convolution_convert_fusion.4 = bf16[768,576]{0,1:T(8,128)(2,1)} fusion(bf16[1024,576]{0,1:T(8,128)(2,1)} %bitcast.249, bf16[1024,768]{1,0:T(8,128)(2,1)S(1)} %bitcast.229), kind=kOutput, calls=%fused_computation.104 | convolution fusion | flops 906412032 | bytes 3637248 | tf_op jit(solution)/shard_map/dot_general | solution.py:78
  159.9 3.9 %multiply_convert_fusion.1 = (bf16[1024,768]{1,0:T(8,128)(2,1)S(1)}, f32[1024,768]{1,0:T(8,128)S(1)}) fusion(f32[768]{0:T(1024)S(1)} %copy-done.39, bf16[1024,768]{1,0:T(8,128)(2,1)S(1)} %bitcast.230, bf16[768,2304]{1,0:T(8,128)(2,1)S(1)} %bitcast.265), kind=kOutput, calls=%fused_computation.96 | convolution fusion | flops 1212678144 | bytes 7475200 | tf_op jit(solution)/shard_map/dot_general | solution.py:551
  163.8 3.0 %fusion.90 = (f32[768]{0:T(1024)S(1)}, bf16[1024,768]{1,0:T(8,128)(2,1)S(1)}) fusion(f32[1024,768]{1,0:T(8,128)S(1)} %get-tuple-element.467, f32[768]{0:T(1024)S(1)} %copy-done.39, bf16[1024,768]{1,0:T(8,128)(2,1)S(1)} %bitcast.226, bf16[768,2304]{1,0:T(8,128)(2,1)S(1)} %bitcast.266), kind=kOutput, calls=%fused_computation.190 | convolution fusion | flops 1217395968 | bytes 7478272 | tf_op jit(solution)/shard_map/dot_general | solution.py:553
  166.8 2.5 convolution_convert_fusion.2
  169.3 2.5 convolution_convert_fusion.3
  173.2 3.2 %pad_maximum_fusion = bf16[768,2304]{0,1:T(8,128)(2,1)} fusion(bf16[768,192]{0,1:T(8,128)(2,1)S(1)} %copy-done.16, bf16[768,576]{0,1:T(8,128)(2,1)} %convolution_convert_fusion.4, bf16[768,768]{0,1:T(8,128)(2,1)S(1)} %copy-done.17, bf16[768,768]{0,1:T(8,128)(2,1)} %convolution_convert_fusion.3), kind=kLoop, calls=%fused_computation.88 | loop fusion | flops 14155776 | bytes 7077888 | tf_op jit(solution)/shard_map/concatenate | solution.py:563
  176.5 5.9 %copy.87 = bf16[768,2304]{1,0:T(8,128)(2,1)} copy(bf16[768,2304]{0,1:T(8,128)(2,1)} %pad_maximum_fusion) | data formatting | bytes 7077888 | tf_op jit(solution)/shard_map/concatenate | solution.py:563
  182.4 2.8 %fusion.61 = f32[1024,768]{1,0:T(8,128)S(1)} fusion(bf16[1024,768]{1,0:T(8,128)(2,1)S(1)} %copy-done.43, bf16[768,2304]{1,0:T(8,128)(2,1)} %bitcast.264), kind=kOutput, calls=%fused_computation.114 | convolution fusion | flops 1207959552 | bytes 5898240 | tf_op jit(solution)/shard_map/dot_general | solution.py:84
  185.3 2.0 add_convert_fusion.1
  188.7 2.6 add_convert_fusion
  191.4 75.5 %scatter_all.1 = (f32[96,2304]{1,0:T(8,128)}, f32[256,768]{1,0:T(8,128)}, f32[256,768]{1,0:T(8,128)}, f32[16,768]{1,0:T(8,128)}) custom-call(bf16[8,96,2304]{2,1,0:T(8,128)(2,1)} %bitcast.233, bf16[4,256,768]{2,1,0:T(8,128)(2,1)} %bitcast.234, bf16[4,256,768]{2,1,0:T(8,128)(2,1)} %bitcast.241, f32[256,768]{1,0:T(8,128)} %get-tuple-element.450.n_ref, ...), custom_call_target="tpu_custom_call" | custom-call | tf_op jit(solution)/shard_map/scatter_all/pallas_call | solution.py:447
  266.9 1.5 multiply_reduce_fusion.2
  268.5 2.6 fusion.69
  (259 shorter events, 75.3 us)
Async XLA Ops:
  0.6 8.6 %copy-start.6 = (bf16[256,768]{1,0:T(8,128)(2,1)S(1)}, bf16[256,768]{1,0:T(8,128)(2,1)}, u32[]{:S(2)}) copy-start(bf16[256,768]{1,0:T(8,128)(2,1)} %param.17) | copy-start | bytes 1179652
  0.7 8.6 %copy-start.27 = (f32[768]{0:T(1024)S(1)}, f32[768]{0:T(1024)}, u32[]{:S(2)}) copy-start(f32[768]{0:T(1024)} %param.20) | copy-start | bytes 9220
  0.7 9.7 %copy-start = (bf16[256,768]{1,0:T(8,128)(2,1)S(1)}, bf16[256,768]{1,0:T(8,128)(2,1)}, u32[]{:S(2)}) copy-start(bf16[256,768]{1,0:T(8,128)(2,1)} %c_ref.1) | copy-start | bytes 1179652
  0.7 8.6 %copy-start.35 = (f32[768]{0:T(1024)S(1)}, f32[768]{0:T(1024)}, u32[]{:S(2)}) copy-start(f32[768]{0:T(1024)} %param.21) | copy-start | bytes 9220
  2.7 7.7 %copy-start.29 = (f32[256]{0:T(256)}, f32[256]{0:T(256)S(1)}, u32[]{:S(2)}) copy-start(f32[256]{0:T(256)S(1)} %broadcast_multiply_fusion.2) | copy-start | bytes 3076
  4.0 6.4 %copy-start.31 = (f32[256]{0:T(256)}, f32[256]{0:T(256)S(1)}, u32[]{:S(2)}) copy-start(f32[256]{0:T(256)S(1)} %add_rsqrt_fusion) | copy-start | bytes 3076
  10.4 64.0 %copy-start.38 = (f32[576]{0:T(1024)S(1)}, f32[576]{0:T(1024)}, u32[]{:S(2)}) copy-start(f32[576]{0:T(1024)} %param.23) | copy-start | bytes 6916
  69.6 4.8 %copy-start.2 = (bf16[4,256,768]{2,1,0:T(8,128)(2,1)S(1)}, bf16[4,256,768]{2,1,0:T(8,128)(2,1)}, u32[]{:S(2)}) copy-start(bf16[4,256,768]{2,1,0:T(8,128)(2,1)} %copy-done.1) | copy-start | bytes 4718596
  82.2 3.1 %copy-start.18 = (bf16[1024,3,48]{0,2,1:T(8,128)(2,1)S(1)}, bf16[1024,3,48]{0,2,1:T(8,128)(2,1)}, u32[]{:S(2)}) copy-start(bf16[1024,3,48]{0,2,1:T(8,128)(2,1)} %slice.318) | copy-start | bytes 884740
  84.5 5.9 %copy-start.23 = (s32[1,1024]{1,0:T(1,128)S(1)}, s32[1,1024]{1,0:T(1,128)}, u32[]{:S(2)}) copy-start(s32[1,1024]{1,0:T(1,128)} %param.19) | copy-start | bytes 12292
  113.7 2.8 copy-start.5
  113.7 3.1 %copy-start.4 = (bf16[3,1024,64]{2,1,0:T(8,128)(2,1)S(1)}, bf16[3,1024,64]{2,1,0:T(8,128)(2,1)}, u32[]{:S(2)}) copy-start(bf16[3,1024,64]{2,1,0:T(8,128)(2,1)} %get-tuple-element.694) | copy-start | bytes 1179652 | tf_op jit(solution)/shard_map/while
  127.9 2.8 copy-start.5
  127.9 3.1 %copy-start.4 = (bf16[3,1024,64]{2,1,0:T(8,128)(2,1)S(1)}, bf16[3,1024,64]{2,1,0:T(8,128)(2,1)}, u32[]{:S(2)}) copy-start(bf16[3,1024,64]{2,1,0:T(8,128)(2,1)} %get-tuple-element.694) | copy-start | bytes 1179652 | tf_op jit(solution)/shard_map/while
  142.1 2.8 copy-start.5
  142.1 3.1 %copy-start.4 = (bf16[3,1024,64]{2,1,0:T(8,128)(2,1)S(1)}, bf16[3,1024,64]{2,1,0:T(8,128)(2,1)}, u32[]{:S(2)}) copy-start(bf16[3,1024,64]{2,1,0:T(8,128)(2,1)} %get-tuple-element.694) | copy-start | bytes 1179652 | tf_op jit(solution)/shard_map/while
  156.5 3.4 %copy-start.25 = (bf16[8,96,2304]{2,1,0:T(8,128)(2,1)S(1)}, bf16[8,96,2304]{2,1,0:T(8,128)(2,1)}, u32[]{:S(2)}) copy-start(bf16[8,96,2304]{2,1,0:T(8,128)(2,1)} %get-tuple-element.215) | copy-start | bytes 10616836
  156.5 3.4 %copy-start.39 = (f32[768]{0:T(1024)S(1)}, f32[768]{0:T(1024)}, u32[]{:S(2)}) copy-start(f32[768]{0:T(1024)} %param.27) | copy-start | bytes 9220
  163.8 3.0 %copy-start.42 = (bf16[1024,768]{1,0:T(8,128)(2,1)}, bf16[1024,768]{1,0:T(8,128)(2,1)S(1)}, u32[]{:S(2)}) copy-start(bf16[1024,768]{1,0:T(8,128)(2,1)S(1)} %get-tuple-element.466) | copy-start | bytes 4718596
  169.3 3.9 %copy-start.16 = (bf16[768,192]{0,1:T(8,128)(2,1)S(1)}, bf16[768,192]{0,1:T(8,128)(2,1)}, u32[]{:S(2)}) copy-start(bf16[768,192]{0,1:T(8,128)(2,1)} %convolution_convert_fusion.6) | copy-start | bytes 884740
  169.3 3.9 %copy-start.17 = (bf16[768,768]{0,1:T(8,128)(2,1)S(1)}, bf16[768,768]{0,1:T(8,128)(2,1)}, u32[]{:S(2)}) copy-start(bf16[768,768]{0,1:T(8,128)(2,1)} %convolution_convert_fusion.2) | copy-start | bytes 3538948
  176.5 5.9 %copy-start.43 = (bf16[1024,768]{1,0:T(8,128)(2,1)S(1)}, bf16[1024,768]{1,0:T(8,128)(2,1)}, u32[]{:S(2)}) copy-start(bf16[1024,768]{1,0:T(8,128)(2,1)} %copy-done.42) | copy-start | bytes 4718596
  182.4 2.9 %copy-start.10 = (bf16[3,1024,64]{1,2,0:T(8,128)(2,1)S(1)}, bf16[3,1024,64]{1,2,0:T(8,128)(2,1)}, u32[]{:S(2)}) copy-start(bf16[3,1024,64]{1,2,0:T(8,128)(2,1)} %get-tuple-element.727) | copy-start | bytes 1179652
  182.4 2.9 %copy-start.26 = (bf16[8,96,2304]{2,1,0:T(8,128)(2,1)S(1)}, bf16[8,96,2304]{2,1,0:T(8,128)(2,1)}, u32[]{:S(2)}) copy-start(bf16[8,96,2304]{2,1,0:T(8,128)(2,1)} %get-tuple-element.215) | copy-start | bytes 10616836
  191.3 75.5 %copy-start.7 = (bf16[256,768]{1,0:T(8,128)(2,1)S(1)}, bf16[256,768]{1,0:T(8,128)(2,1)}, u32[]{:S(2)}) copy-start(bf16[256,768]{1,0:T(8,128)(2,1)} %param.17) | copy-start | bytes 1179652
  191.3 75.6 %copy-start.28 = (f32[768]{0:T(1024)S(1)}, f32[768]{0:T(1024)}, u32[]{:S(2)}) copy-start(f32[768]{0:T(1024)} %param.20) | copy-start | bytes 9220
  191.3 75.6 %copy-start.30 = (f32[256]{0:T(256)S(1)}, f32[256]{0:T(256)}, u32[]{:S(2)}) copy-start(f32[256]{0:T(256)} %copy-done.29) | copy-start | bytes 3076
  191.3 75.6 %copy-start.32 = (f32[256]{0:T(256)S(1)}, f32[256]{0:T(256)}, u32[]{:S(2)}) copy-start(f32[256]{0:T(256)} %copy-done.31) | copy-start | bytes 3076
  191.3 77.1 %copy-start.36 = (f32[768]{0:T(1024)S(1)}, f32[768]{0:T(1024)}, u32[]{:S(2)}) copy-start(f32[768]{0:T(1024)} %param.29) | copy-start | bytes 9220
  191.3 77.1 %copy-start.37 = (f32[768]{0:T(1024)S(1)}, f32[768]{0:T(1024)}, u32[]{:S(2)}) copy-start(f32[768]{0:T(1024)} %param.25) | copy-start | bytes 9220
  266.9 7.7 %copy-start.21 = (f32[96,2304]{1,0:T(8,128)S(1)}, f32[96,2304]{1,0:T(8,128)}, u32[]{:S(2)}) copy-start(f32[96,2304]{1,0:T(8,128)} %get-tuple-element.224) | copy-start | bytes 2654212
  273.3 4.3 %copy-start.33 = (f32[768]{0:T(1024)}, f32[768]{0:T(1024)S(1)}, u32[]{:S(2)}) copy-start(f32[768]{0:T(1024)S(1)} %get-tuple-element.723) | copy-start | bytes 9220
  (22 other events, 37.5 us)

commit v3 on v2

--- a/solution.py
+++ b/solution.py
@@ -56,24 +56,6 @@
     )
 
 
-def rotate(tensor, cos_table, sin_table):
-    halves = ROT // 2
-    turned_part = tensor[..., :ROT]
-    turned = jnp.concatenate([-turned_part[..., halves:], turned_part[..., :halves]], axis=-1)
-    spun = turned_part * cos_table[:, None, :] + turned * sin_table[:, None, :]
-    return jnp.concatenate([spun, tensor[..., ROT:]], axis=-1)
-
-
-def unrotate(grad_in, cos_table, sin_table):
-    halves = ROT // 2
-    turned_part = grad_in[..., :ROT]
-    scaled = turned_part * sin_table[:, None, :]
-    back = jnp.concatenate([scaled[..., halves:], -scaled[..., :halves]], axis=-1)
-    return jnp.concatenate(
-        [turned_part * cos_table[:, None, :] + back, grad_in[..., ROT:]], axis=-1
-    )
-
-
 def cross_rows(left, right):
     return lax.dot_general(
         left, right, (((0,), (0,)), ((), ())), preferred_element_type=jnp.float32
@@ -84,67 +66,6 @@
     return lax.dot_general(
         left, right, (((1,), (1,)), ((), ())), preferred_element_type=jnp.float32
     )
-
-
-def block_scores(queries, keys_in, segment_row, first_row, last_row, score_scale):
-    counter = jnp.arange(last_row, dtype=jnp.int32)
-    allowed = (segment_row[first_row:last_row, None] == segment_row[None, :last_row]) & (
-        counter[first_row:last_row, None] >= counter[None, :last_row]
-    )
-    scores = cross_cols(queries[first_row:last_row], keys_in[:last_row]) * score_scale
-    return jnp.where(allowed, scores, -jnp.inf)
-
-
-def head_forward(queries, keys_in, values_in, segment_row, score_scale):
-    length = queries.shape[0]
-    span = min(512, length)
-    mixed_parts = []
-    total_parts = []
-    for first_row in range(0, length, span):
-        last_row = min(first_row + span, length)
-        scores = block_scores(queries, keys_in, segment_row, first_row, last_row, score_scale)
-        highest = jnp.max(scores, axis=-1, keepdims=True)
-        log_total = highest + jnp.log(jnp.sum(jnp.exp(scores - highest), axis=-1, keepdims=True))
-        weights = jnp.exp(scores - log_total).astype(jnp.bfloat16)
-        mixed_parts.append(
-            jnp.dot(weights, values_in[:last_row], preferred_element_type=jnp.float32).astype(
-                jnp.bfloat16
-            )
-        )
-        total_parts.append(log_total)
-    return (jnp.concatenate(mixed_parts, axis=0), jnp.concatenate(total_parts, axis=0))
-
-
-def head_backward(
-    queries, keys_in, values_in, mixed, grad_mixed, log_total, segment_row, score_scale
-):
-    length = queries.shape[0]
-    span = min(512, length)
-    delta = jnp.sum(
-        grad_mixed.astype(jnp.float32) * mixed.astype(jnp.float32), axis=-1, keepdims=True
-    )
-    grad_keys = jnp.zeros(keys_in.shape, jnp.float32)
-    grad_values = jnp.zeros(values_in.shape, jnp.float32)
-    query_parts = []
-    for first_row in range(0, length, span):
-        last_row = min(first_row + span, length)
-        padding = ((0, length - last_row), (0, 0))
-        scores = block_scores(queries, keys_in, segment_row, first_row, last_row, score_scale)
-        probs = jnp.exp(scores - log_total[first_row:last_row])
-        weights = probs.astype(jnp.bfloat16)
-        grad_rows = grad_mixed[first_row:last_row]
-        grad_values = grad_values + jnp.pad(cross_rows(weights, grad_rows), padding)
-        grad_probs = cross_cols(grad_rows, values_in[:last_row])
-        grad_scores = (probs * (grad_probs - delta[first_row:last_row]) * score_scale).astype(
-            jnp.bfloat16
-        )
-        query_parts.append(
-            jnp.dot(grad_scores, keys_in[:last_row], preferred_element_type=jnp.float32)
-        )
-        grad_keys = grad_keys + jnp.pad(
-            cross_rows(grad_scores, queries[first_row:last_row]), padding
-        )
-    return (jnp.concatenate(query_parts, axis=0), grad_keys, grad_values)
 
 
 MESH = pl.DeviceIdType.MESH
@@ -293,34 +214,31 @@
 def scatter_kernel(
     fsdp,
     tp,
-    g_ref,
-    b_ref,
-    d_ref,
-    n_ref,
-    v_ref,
-    g_out,
-    b_out,
-    d_out,
-    v_out,
-    halves,
-    joined,
-    lands,
-    b_land,
-    d_land,
-    rows,
-    first,
-    second,
-    p_send,
-    p_recv,
-    w_send,
-    w_recv,
-    r_send,
-    r_recv,
-    v_send,
-    v_recv,
-    u_send,
-    u_recv,
+    many,
+    *refs,
 ):
+    g_refs, refs = refs[:many], refs[many:]
+    b_ref, d_ref, n_ref, v_ref = refs[:4]
+    g_outs, refs = refs[4 : 4 + many], refs[4 + many :]
+    b_out, d_out, v_out = refs[:3]
+    halves, joined, lands = (refs[3 + many * i : 3 + many * (i + 1)] for i in range(3))
+    (
+        b_land,
+        d_land,
+        rows,
+        first,
+        second,
+        p_send,
+        p_recv,
+        w_send,
+        w_recv,
+        r_send,
+        r_recv,
+        v_send,
+        v_recv,
+        u_send,
+        u_recv,
+    ) = refs[3 + 3 * many :]
     f, t, pair, line = place(fsdp, tp)
     lines = fsdp // 2
     greet(fsdp, tp)
@@ -329,21 +247,21 @@
     def ahead(step):
         return lax.rem(line + step, lines)
 
-    def across(step):
+    def across(i, step):
         return remote(
-            g_ref.at[2 * ahead(step) + 1 - pair],
-            halves.at[step],
-            p_send.at[step],
-            p_recv.at[step],
+            g_refs[i].at[2 * ahead(step) + 1 - pair],
+            halves[i].at[step],
+            p_send.at[i, step],
+            p_recv.at[i, step],
             (partner, t),
         )
 
-    def along(step):
+    def along(i, step):
         return remote(
-            joined.at[step],
-            lands.at[step],
-            w_send.at[step],
-            w_recv.at[step],
+            joined[i].at[step],
+            lands[i].at[step],
+            w_send.at[i, step],
+            w_recv.at[i, step],
             (2 * ahead(step) + pair, t),
         )
 
@@ -360,21 +278,27 @@
         beside(step, 1, d_ref, d_land).start()
         beside(step, 0, b_ref, b_land).start()
 
-    each(1, lines, lambda step: across(step).start())
-    across(0).start()
+    def start_across(step):
+        for i in range(many):
+            across(i, step).start()
+
+    each(1, lines, start_across)
+    start_across(0)
     each(1, tp, start_beside)
 
     def join(step):
-        across(step).wait_recv()
-        joined[step] = (
-            g_ref[2 * ahead(step) + pair].astype(jnp.float32)
-            + halves[step].astype(jnp.float32)
-        ).astype(joined.dtype)
-        along(step).start()
+        for i in range(many):
+            across(i, step).wait_recv()
+            joined[i][step] = (
+                g_refs[i][2 * ahead(step) + pair].astype(jnp.float32)
+                + halves[i][step].astype(jnp.float32)
+            ).astype(joined[i].dtype)
+            along(i, step).start()
 
     each(1, lines, join)
-    across(0).wait_recv()
-    g_out[...] = g_ref[f].astype(jnp.float32) + halves[0].astype(jnp.float32)
+    for i in range(many):
+        across(i, 0).wait_recv()
+        g_outs[i][...] = g_refs[i][f].astype(jnp.float32) + halves[i][0].astype(jnp.float32)
 
     d_out[...] = d_ref[t].astype(jnp.float32)
     b_out[...] = b_ref[t].astype(jnp.float32)
@@ -406,8 +330,9 @@
     each(1, tp, gather_b)
 
     def collect(step):
-        along(step).wait_recv()
-        g_out[...] += lands[step].astype(jnp.float32)
+        for i in range(many):
+            along(i, step).wait_recv()
+            g_outs[i][...] += lands[i][step].astype(jnp.float32)
 
     each(1, lines, collect)
     each(1, fsdp, lambda step: spread(step, lax.rem(f + fsdp - step, fsdp)).wait())
@@ -425,8 +350,17 @@
         )
 
     each(1, tp, lambda step: share(step, t).start())
-    each(1, lines, lambda step: along(step).wait_send())
-    each(0, lines, lambda step: across(step).wait_send())
+
+    def sent_along(step):
+        for i in range(many):
+            along(i, step).wait_send()
+
+    def sent_across(step):
+        for i in range(many):
+            across(i, step).wait_send()
+
+    each(1, lines, sent_along)
+    each(0, lines, sent_across)
     each(1, tp, lambda step: share(step, lax.rem(t + tp - step, tp)).wait())
     whole = second[0]
     for step in range(1, tp):
@@ -438,35 +372,38 @@
     fsdp = lax.axis_size("fsdp")
     tp = lax.axis_size("tp")
     lines = fsdp // 2
-    grads = grads.reshape(fsdp, -1, grads.shape[1])
+    grads = [grad.reshape(fsdp, -1, grad.shape[1]) for grad in grads]
+    many = len(grads)
     branch = branch.reshape(tp, -1, branch.shape[1])
     feature_grad = feature_grad.reshape(tp, -1, feature_grad.shape[1])
     vmem = pl.BlockSpec(memory_space=pltpu.VMEM)
     dma = pltpu.SemaphoreType.DMA
     f32 = jnp.float32
     return pl.pallas_call(
-        functools.partial(scatter_kernel, fsdp, tp),
+        functools.partial(scatter_kernel, fsdp, tp, many),
         out_shape=(
-            jax.ShapeDtypeStruct(grads.shape[1:], f32),
+            *(jax.ShapeDtypeStruct(grad.shape[1:], f32) for grad in grads),
             jax.ShapeDtypeStruct(branch.shape[1:], f32),
             jax.ShapeDtypeStruct(feature_grad.shape[1:], f32),
             jax.ShapeDtypeStruct(vectors.shape, f32),
         ),
-        in_specs=[vmem] * 5,
-        out_specs=(vmem,) * 4,
+        in_specs=[vmem] * (many + 4),
+        out_specs=(vmem,) * (many + 3),
         scratch_shapes=[
-            pltpu.VMEM((lines,) + grads.shape[1:], grads.dtype),
-            pltpu.VMEM((lines,) + grads.shape[1:], grads.dtype),
-            pltpu.VMEM((lines,) + grads.shape[1:], grads.dtype),
+            *(
+                pltpu.VMEM((lines,) + grad.shape[1:], grad.dtype)
+                for _ in range(3)
+                for grad in grads
+            ),
             pltpu.VMEM(branch.shape, branch.dtype),
             pltpu.VMEM(feature_grad.shape, feature_grad.dtype),
             pltpu.VMEM(vectors.shape, f32),
             pltpu.VMEM((fsdp,) + vectors.shape, f32),
             pltpu.VMEM((tp, 8, vectors.shape[1]), f32),
-            dma((lines,)),
-            dma((lines,)),
-            dma((lines,)),
-            dma((lines,)),
+            dma((many, lines)),
+            dma((many, lines)),
+            dma((many, lines)),
+            dma((many, lines)),
             dma((2, tp)),
             dma((2, tp)),
             dma((fsdp,)),
@@ -478,46 +415,145 @@
             collective_id=2, has_side_effects=True, vmem_limit_bytes=56 * 1024 * 1024
         ),
         name="scatter_all",
-    )(grads, branch, feature_grad, normed, vectors)
+    )(*grads, branch, feature_grad, normed, vectors)
+
+
+MOST = 512
+SPAN = 256
+
+
+def attention_kernel(
+    heads,
+    x_ref,
+    do_ref,
+    cos_ref,
+    sin_ref,
+    turn_ref,
+    col_ref,
+    row_ref,
+    o_ref,
+    dx_ref,
+    sum_ref,
+    queries,
+    keys_in,
+    values_in,
+    grads_in,
+    mixed,
+    grad_q,
+    grad_k,
+    grad_v,
+):
+    length = x_ref.shape[0]
+    span = min(SPAN, length)
+    scale = HEAD_DIM ** (-0.5)
+    two = 2 * HEAD_DIM
+    f32 = jnp.float32
+    bf16 = jnp.bfloat16
+
+    def turned(value, axis):
+        return lax.dot_general(
+            value,
+            turn_ref[...],
+            (((1,), (axis,)), ((), ())),
+            precision=lax.Precision.HIGHEST,
+            preferred_element_type=f32,
+        )
+
+    for n in range(heads):
+        base = 3 * HEAD_DIM * n
+        for first in range(0, length, span):
+            part = slice(first, first + span)
+            both = x_ref[part, base : base + two]
+            both = both * cos_ref[part] + turned(both, 0) * sin_ref[part]
+            queries[n, part] = both[:, :HEAD_DIM].astype(bf16) * bf16(scale)
+            keys_in[n, part] = both[:, HEAD_DIM:].astype(bf16)
+            values_in[n, part] = x_ref[part, base + two : base + two + HEAD_DIM].astype(bf16)
+            grads_in[n, part] = do_ref[part, n * HEAD_DIM : (n + 1) * HEAD_DIM]
+    grad_k[...] = jnp.zeros_like(grad_k)
+    grad_v[...] = jnp.zeros_like(grad_v)
+
+    def one_head(n, carry):
+        for first in range(0, length, span):
+            last = first + span
+            low = max(0, (first - MOST) // span * span)
+            part = slice(first, last)
+            window = slice(low, last)
+            q = queries[n, part]
+            k = keys_in[n, window]
+            v = values_in[n, window]
+            g = grads_in[n, part]
+            shape = (span, last - low)
+            allowed = (col_ref[part] == row_ref[:, window]) & (
+                lax.broadcasted_iota(jnp.int32, shape, 0) + first
+                >= lax.broadcasted_iota(jnp.int32, shape, 1) + low
+            )
+            scores = jnp.where(allowed, cross_cols(q, k), -1e30)
+            exps = jnp.exp(scores - jnp.max(scores, axis=-1, keepdims=True))
+            probs = exps * (1.0 / jnp.sum(exps, axis=-1, keepdims=True))
+            weights = probs.astype(bf16)
+            out = jnp.dot(weights, v, preferred_element_type=f32).astype(bf16)
+            mixed[n, part] = out
+            delta = jnp.sum(g.astype(f32) * out.astype(f32), axis=-1, keepdims=True)
+            grad_probs = cross_cols(g, v)
+            grad_scores = (probs * (grad_probs - delta)).astype(bf16)
+            grad_q[n, part] = jnp.dot(grad_scores, k, preferred_element_type=f32) * scale
+            grad_k[n, window] += cross_rows(grad_scores, q)
+            grad_v[n, window] += cross_rows(weights, g)
+        return carry
+
+    lax.fori_loop(0, heads, one_head, 0)
+
+    sum_ref[...] = jnp.zeros_like(sum_ref)
+    for first in range(0, length, span):
+        part = slice(first, first + span)
+        pieces = []
+        for n in range(heads):
+            both = jnp.concatenate([grad_q[n, part], grad_k[n, part]], axis=1)
+            both = both * cos_ref[part] + turned(both * sin_ref[part], 1)
+            pieces += [both, grad_v[n, part]]
+        whole = jnp.concatenate(pieces, axis=1)
+        sum_ref[...] += jnp.sum(whole, axis=0, keepdims=True)
+        dx_ref[part] = whole.astype(bf16)
+        o_ref[part] = jnp.concatenate([mixed[n, part] for n in range(heads)], axis=1)
 
 
 def attention_branch(features, grad_rows, qkv_full, qkv_bias, out_full, segment_row):
-    score_scale = HEAD_DIM ** (-0.5)
     length = features.shape[0]
-    local_heads = qkv_full.shape[1] // (3 * HEAD_DIM)
+    heads = qkv_full.shape[1] // (3 * HEAD_DIM)
     cos_table, sin_table = rotary_tables(positions_of(segment_row))
-    packed = (jnp.dot(features, qkv_full, preferred_element_type=jnp.float32) + qkv_bias).reshape(
-        length, local_heads, 3, HEAD_DIM
-    )
-    queries = rotate(packed[:, :, 0], cos_table, sin_table).astype(jnp.bfloat16).transpose(1, 0, 2)
-    keys_all = rotate(packed[:, :, 1], cos_table, sin_table).astype(jnp.bfloat16).transpose(1, 0, 2)
-    values_all = packed[:, :, 2].astype(jnp.bfloat16).transpose(1, 0, 2)
-
-    def forward_head(member):
-        return head_forward(member[0], member[1], member[2], segment_row, score_scale)
-
-    mixed, log_total = lax.map(forward_head, (queries, keys_all, values_all))
-    mixed_rows = mixed.transpose(1, 0, 2).reshape(length, local_heads * HEAD_DIM)
-    mixed_grad = (
-        jnp.dot(grad_rows, out_full, preferred_element_type=jnp.float32)
-        .astype(jnp.bfloat16)
-        .reshape(length, local_heads, HEAD_DIM)
-        .transpose(1, 0, 2)
-    )
-
-    def backward_head(member):
-        return head_backward(*member, segment_row, score_scale)
-
-    grad_q, grad_k, grad_v = lax.map(
-        backward_head, (queries, keys_all, values_all, mixed, mixed_grad, log_total)
-    )
-    grad_q = unrotate(grad_q.transpose(1, 0, 2), cos_table, sin_table)
-    grad_k = unrotate(grad_k.transpose(1, 0, 2), cos_table, sin_table)
-    grad_v = grad_v.transpose(1, 0, 2)
-    packed_grad = jnp.stack([grad_q, grad_k, grad_v], axis=2).reshape(
-        length, 3 * local_heads * HEAD_DIM
-    )
-    return mixed_rows, packed_grad.astype(jnp.bfloat16), jnp.sum(packed_grad, axis=0)
+    rest = ((0, 0), (0, HEAD_DIM - ROT))
+    cos_full = jnp.tile(jnp.pad(cos_table, rest, constant_values=1.0), (1, 2))
+    sin_full = jnp.tile(jnp.pad(sin_table, rest), (1, 2))
+    half = ROT // 2
+    source = jnp.arange(2 * HEAD_DIM)[:, None]
+    target = jnp.arange(2 * HEAD_DIM)[None, :]
+    inner = target % HEAD_DIM
+    turn = jnp.where(
+        (inner < half) & (source == target + half),
+        -1.0,
+        jnp.where((inner >= half) & (inner < ROT) & (source == target - half), 1.0, 0.0),
+    ).astype(jnp.float32)
+    packed = jnp.dot(features, qkv_full, preferred_element_type=jnp.float32) + qkv_bias
+    mixed_grad = jnp.dot(grad_rows, out_full, preferred_element_type=jnp.float32).astype(
+        jnp.bfloat16
+    )
+    wide = packed.shape[1]
+    vmem = pl.BlockSpec(memory_space=pltpu.VMEM)
+    mixed_rows, packed_grad, sums = pl.pallas_call(
+        functools.partial(attention_kernel, heads),
+        out_shape=(
+            jax.ShapeDtypeStruct((length, heads * HEAD_DIM), jnp.bfloat16),
+            jax.ShapeDtypeStruct((length, wide), jnp.bfloat16),
+            jax.ShapeDtypeStruct((1, wide), jnp.float32),
+        ),
+        in_specs=[vmem] * 7,
+        out_specs=(vmem,) * 3,
+        scratch_shapes=[pltpu.VMEM((heads, length, HEAD_DIM), jnp.bfloat16)] * 5
+        + [pltpu.VMEM((heads, length, HEAD_DIM), jnp.float32)] * 3,
+        compiler_params=pltpu.CompilerParams(vmem_limit_bytes=56 * 1024 * 1024),
+        name="attention",
+    )(packed, mixed_grad, cos_full, sin_full, turn, segment_row[:, None], segment_row[None, :])
+    return mixed_rows, packed_grad, sums[0]
 
 
 def body(
@@ -560,15 +596,12 @@
     )
     branch = cross_cols(mixed_rows, full_out) + cross_cols(gelu_rows, full_down)
     feature_grad = cross_cols(packed_bf, full_qkv) + cross_cols(pre_grads, full_up)
-    grads = jnp.concatenate(
-        [
-            cross_rows(features, pre_grads).astype(jnp.bfloat16),
-            cross_rows(grad_rows, gelu_rows).astype(jnp.bfloat16),
-            cross_rows(features, packed_bf).astype(jnp.bfloat16),
-            cross_rows(grad_rows, mixed_rows).astype(jnp.bfloat16),
-        ],
-        axis=1,
-    )
+    grads = [
+        cross_rows(features, pre_grads).astype(jnp.bfloat16),
+        cross_rows(grad_rows, gelu_rows).astype(jnp.bfloat16),
+        cross_rows(features, packed_bf).astype(jnp.bfloat16),
+        cross_rows(grad_rows, mixed_rows).astype(jnp.bfloat16),
+    ]
     cot_rows = out_cotangent.astype(jnp.float32)
     model = own_rows.shape[1]
     biases = jnp.concatenate([qkv_bias_part, up_bias_part])
@@ -583,7 +616,7 @@
             jnp.zeros((-bias_rows % 8, model), jnp.float32),
         ]
     )
-    grad_sum, branch, row_grad, sums = scatter_all(
+    up_grad, down_grad, qkv_grad, out_grad, branch, row_grad, sums = scatter_all(
         grads,
         branch.astype(jnp.bfloat16),
         feature_grad.astype(jnp.bfloat16),
@@ -605,7 +638,6 @@
             - normed * jnp.mean(scaled * normed, axis=-1, keepdims=True)
         )
     ).astype(jnp.bfloat16)
-    up_grad, down_grad, qkv_grad, out_grad = jnp.split(grad_sum, ends, axis=1)
     return (
         layer_output,
         input_grad,

time: 280 us -> 219 us (0.78)
  matrix products: 62.4 us -> 34.1 us
  local copies, waits for them, and re-layouts: 49 us -> 21.6 us
  other arithmetic: 31.1 us -> 11.7 us
  Pallas kernels: 134 us -> 149 us
    dot_general x22 -> x4, matrix products: 27.1 us -> 9.24 us  [cross_cols(): lax.dot_general(left, right, (((1,), (1,)), ((), ())), preferred_element_...]
    pallas_call x1 -> x2, Pallas kernels: 75.5 us -> 91.6 us  [the longest x1 72.5 us: scatter_all(): pl.pallas_call(functools.partial(scatter_kernel, fsdp, tp, many), out_sha...]
    dynamic_slice x6 -> x0, local copies, waits for them, and re-layouts: 9.93 us -> none  [attention_branch(): mixed, log_total = lax.map(forward_head, (queries, keys_all, values_all))]
    while x33 -> x0, local copies, waits for them, and re-layouts: 8.08 us -> none  [the longest x2 4.33 us: attention_branch(): lax.map(backward_head, (queries, keys_all, values_all, mixed, mixed_grad,...]
    dot_general x16 -> x4, matrix products: 18.7 us -> 10.8 us  [cross_rows(): lax.dot_general(left, right, (((0,), (0,)), ((), ())), preferred_element_...]
    slice x23 -> x1, local copies, waits for them, and re-layouts: 7.26 us -> 0.07 us  [the longest x3 3.79 us: head_backward(): probs = jnp.exp(scores - log_total[first_row:last_row])]
    reduce_sum x10 -> x0, other arithmetic: 6.41 us -> none  [the longest x3 4.08 us: head_backward(): jnp.sum(grad_mixed.astype(jnp.float32) * mixed.astype(jnp.float32), axis=...]
    dynamic_update_slice x9 -> x0, other arithmetic: 5.97 us -> none  [the longest x6 3.8 us: attention_branch(): mixed, log_total = lax.map(forward_head, (queries, keys_all, values_all))]
where the time goes in v3:
time: 219 us; the launch traced here: 218 us
  Pallas kernels  149 us (68%)
  matrix products  34.1 us (16%)
  local copies, waits for them, and re-layouts  21.6 us (10%)
  other arithmetic  11.7 us (5%)
    pallas_call x1, Pallas kernels, scatter_all(): pl.pallas_call(functools.partial(scatter_kernel, fsdp, tp, many), out_sha...  72.5 us
    pallas_call x1, Pallas kernels, gather_all(): pl.pallas_call(functools.partial(gather_kernel, fsdp, tp), out_shape=shap...  57.8 us
    pallas_call x1, Pallas kernels, attention_branch(): pl.pallas_call(functools.partial(attention_kernel, heads), out_shape=(jax...  19.1 us
    dot_general x4, matrix products, cross_rows(): lax.dot_general(left, right, (((0,), (0,)), ((), ())), preferred_element_...  10.8 us
    dot_general x4, matrix products, cross_cols(): lax.dot_general(left, right, (((1,), (1,)), ((), ())), preferred_element_...  9.24 us
    unnamed x54, local copies, waits for them, and re-layouts  5.6 us

profile of v3, /device:TPU:0, one launch (start us, length us, event | category | flops | bytes accessed | tf_op | source)
XLA Modules:
  0.0 217.8 jit_solution(17295944801686013769)
XLA Ops:
  1.5 1.1 convert_reduce_fusion
  2.7 1.2 fusion.16
  4.6 1.1 convert_reduce_fusion.1
  6.2 0.9 copy.40
  8.0 1.1 concatenate.20.w_ref
  9.3 1.0 copy.45.sin_ref
  10.4 1.0 copy.44.cos_ref
  11.4 1.1 copy.46.col_ref
  12.5 1.1 fusion.12
  13.6 57.8 %gather_all.1 = (bf16[8,96,2304]{2,1,0:T(8,128)(2,1)}, bf16[4,256,768]{2,1,0:T(8,128)(2,1)S(1)}, bf16[4,256,768]{2,1,0:T(8,128)(2,1)S(1)}) custom-call(bf16[96,2304]{1,0:T(8,128)(2,1)S(1)} %concatenate.20.w_ref, bf16[256,768]{1,0:T(8,128)(2,1)S(1)} %get-tuple-element.80.h_ref, bf16[256,768]{1,0:T(8,128)(2,1)S(1)} %copy-done), custom_call_target="tpu_custom_call" | custom-call | tf_op jit(solution)/shard_map/gather_all/pallas_call | solution.py:189
  71.5 1.2 copy-done.1
  72.6 2.6 %convolution_convert_fusion.3 = bf16[1024,192]{0,1:T(8,128)(2,1)} fusion(bf16[1024,768]{1,0:T(8,128)(2,1)S(1)} %bitcast.40, bf16[768,2304]{1,0:T(8,128)(2,1)} %bitcast.58), kind=kOutput, calls=%fused_computation.14 | convolution fusion | flops 302186496 | bytes 2359296 | tf_op jit(solution)/shard_map/dot_general | solution.py:537
  75.3 2.0 copy.43.do_ref
  77.3 4.1 %convolution_add_fusion.x_ref = f32[1024,576]{1,0:T(8,128)} fusion(bf16[1024,768]{1,0:T(8,128)(2,1)S(1)} %bitcast.44, f32[576]{0:T(1024)S(1)} %copy-done.19, bf16[768,2304]{1,0:T(8,128)(2,1)} %bitcast.59), kind=kOutput, calls=%fused_computation.10 | convolution fusion | flops 906559488 | bytes 4917504 | tf_op jit(solution)/shard_map/dot_general | solution.py:536
  81.4 19.1 %attention.1 = (bf16[1024,192]{1,0:T(8,128)(2,1)}, bf16[1024,576]{1,0:T(8,128)(2,1)}, f32[1,576]{1,0:T(1,128)}) custom-call(f32[1024,576]{1,0:T(8,128)} %convolution_add_fusion.x_ref, bf16[1024,192]{1,0:T(8,128)(2,1)} %copy.43.do_ref, f32[1024,128]{1,0:T(8,128)} %copy.44.cos_ref, f32[1024,128]{1,0:T(8,128)} %copy.45.sin_ref, ...), custom_call_target="tpu_custom_call" | custom-call | tf_op jit(solution)/shard_map/attention/pallas_call | solution.py:542
  101.2 2.3 %convolution_convert_fusion.4 = bf16[768,192]{0,1:T(8,128)(2,1)} fusion(bf16[1024,768]{1,0:T(8,128)(2,1)S(1)} %bitcast.41, bf16[1024,192]{1,0:T(8,128)(2,1)} %get-tuple-element.29), kind=kOutput, calls=%fused_computation.15 | convolution fusion | flops 302137344 | bytes 2260992 | tf_op jit(solution)/shard_map/dot_general | solution.py:60
  103.5 1.9 copy.48
  105.3 3.5 %convolution_convert_fusion.2 = bf16[768,576]{0,1:T(8,128)(2,1)} fusion(bf16[1024,768]{1,0:T(8,128)(2,1)S(1)} %bitcast.45, bf16[1024,576]{1,0:T(8,128)(2,1)} %get-tuple-element.28), kind=kOutput, calls=%fused_computation.13 | convolution fusion | flops 906412032 | bytes 3637248 | tf_op jit(solution)/shard_map/dot_general | solution.py:60
  108.8 2.2 %copy.47 = bf16[768,576]{1,0:T(8,128)(2,1)} copy(bf16[768,576]{0,1:T(8,128)(2,1)} %convolution_convert_fusion.2) | data formatting | bytes 1769472 | tf_op jit(solution)/shard_map/convert_element_type | solution.py:602
  111.0 3.2 %multiply_convert_fusion = (bf16[1024,768]{1,0:T(8,128)(2,1)S(1)}, f32[1024,768]{1,0:T(8,128)S(1)}) fusion(f32[768]{0:T(1024)} %param.23, bf16[1024,768]{1,0:T(8,128)(2,1)S(1)} %bitcast.46, bf16[768,2304]{1,0:T(8,128)(2,1)} %bitcast.60), kind=kOutput, calls=%fused_computation.8 | convolution fusion | flops 1212678144 | bytes 7475200 | tf_op jit(solution)/shard_map/dot_general | solution.py:587
  114.3 4.1 %fusion.28 = (f32[768]{0:T(1024)S(1)}, bf16[1024,768]{1,0:T(8,128)(2,1)S(1)}) fusion(f32[1024,768]{1,0:T(8,128)S(1)} %get-tuple-element.86, f32[768]{0:T(1024)S(1)} %copy-done.20, bf16[1024,768]{1,0:T(8,128)(2,1)S(1)} %bitcast.42, bf16[768,2304]{1,0:T(8,128)(2,1)} %bitcast.61), kind=kOutput, calls=%fused_computation.75 | convolution fusion | flops 1217395968 | bytes 7477248 | tf_op jit(solution)/shard_map/dot_general | solution.py:589
  118.4 2.5 %convolution_convert_fusion = bf16[768,768]{1,0:T(8,128)(2,1)} fusion(bf16[1024,768]{1,0:T(8,128)(2,1)S(1)} %bitcast.43, bf16[1024,768]{1,0:T(8,128)(2,1)S(1)} %get-tuple-element.85), kind=kOutput, calls=%fused_computation.11 | convolution fusion | flops 1208549376 | bytes 4325376 | tf_op jit(solution)/shard_map/dot_general | solution.py:60
  120.9 2.6 %convolution_convert_fusion.1 = bf16[768,768]{1,0:T(8,128)(2,1)} fusion(bf16[1024,768]{1,0:T(8,128)(2,1)S(1)} %bitcast.47, bf16[1024,768]{1,0:T(8,128)(2,1)S(1)} %get-tuple-element.88), kind=kOutput, calls=%fused_computation.12 | convolution fusion | flops 1208549376 | bytes 4325376 | tf_op jit(solution)/shard_map/dot_general | solution.py:60
  123.6 1.3 concatenate.26.refs_7_
  124.8 3.3 %fusion.9 = f32[1024,768]{1,0:T(8,128)S(1)} fusion(bf16[1024,768]{1,0:T(8,128)(2,1)} %copy-done.23, bf16[768,2304]{1,0:T(8,128)(2,1)} %bitcast.62), kind=kOutput, calls=%fused_computation.23 | convolution fusion | flops 1207959552 | bytes 5898240 | tf_op jit(solution)/shard_map/dot_general | solution.py:66
  128.2 1.9 add_convert_fusion.1
  130.1 1.4 fusion.5
  131.5 2.6 %add_convert_fusion = bf16[1024,768]{1,0:T(8,128)(2,1)} fusion(f32[1024,768]{1,0:T(8,128)S(1)} %fusion.5, bf16[1024,576]{1,0:T(8,128)(2,1)S(1)} %copy-done.18, bf16[768,2304]{1,0:T(8,128)(2,1)S(1)} %bitcast.65), kind=kOutput, calls=%fused_computation.6 | convolution fusion | flops 907542528 | bytes 7012352 | tf_op jit(solution)/shard_map/dot_general | solution.py:66
  134.1 72.5 %scatter_all.1 = (f32[96,768]{1,0:T(8,128)}, f32[96,768]{1,0:T(8,128)}, f32[96,576]{1,0:T(8,128)}, f32[96,192]{1,0:T(8,128)}, f32[256,768]{1,0:T(8,128)}, /*index=5*/f32[256,768]{1,0:T(8,128)}, f32[16,768]{1,0:T(8,128)}) custom-call(bf16[8,96,768]{2,1,0:T(8,128)(2,1)} %bitcast.55, bf16[8,96,768]{2,1,0:T(8,128)(2,1)} %bitcast.54, ...), custom_call_target="tpu_custom_call" | custom-call | tf_op jit(solution)/shard_map/scatter_all/pallas_call | solution.py:382
  206.6 1.4 multiply_reduce_fusion.1
  208.2 2.7 %fusion.17 = (bf16[256,768]{1,0:T(8,128)(2,1)}, bf16[256,768]{1,0:T(8,128)(2,1)}) fusion(bf16[256,768]{1,0:T(8,128)(2,1)S(1)} %copy-done, f32[256,768]{1,0:T(8,128)} %get-tuple-element.32, f32[256]{0:T(256)S(1)} %broadcast_multiply_fusion, f32[256]{0:T(256)S(1)} %broadcast_multiply_fusion.1, f32[768]{0:T(1024)S(1)} %copy-done.12, f32[256]{0:T(256)S(1)} %add_rsqrt_fusion, ...), kind=kLoop, calls=%fused_computation.33 | loop fusion | flops 2949120 | bytes 3159040 | tf_op jit(solution)/shard_map/convert_element_type | solution.py:640
  211.6 1.5 slice_reduce_fusion.1
  (82 shorter events, 9.5 us)
Async XLA Ops:
  9.2 2.2 %copy-start.11 = (s32[1,1024]{1,0:T(1,128)S(1)}, s32[1,1024]{1,0:T(1,128)}, u32[]{:S(2)}) copy-start(s32[1,1024]{1,0:T(1,128)} %row_ref.1) | copy-start | bytes 12292
  9.2 3.2 %copy-start.3 = (bf16[256,768]{1,0:T(8,128)(2,1)S(1)}, bf16[256,768]{1,0:T(8,128)(2,1)}, u32[]{:S(2)}) copy-start(bf16[256,768]{1,0:T(8,128)(2,1)} %param.13) | copy-start | bytes 1179652
  9.3 3.2 %copy-start.12 = (f32[768]{0:T(1024)S(1)}, f32[768]{0:T(1024)}, u32[]{:S(2)}) copy-start(f32[768]{0:T(1024)} %param.16) | copy-start | bytes 9220
  9.3 3.2 %copy-start.15 = (f32[768]{0:T(1024)S(1)}, f32[768]{0:T(1024)}, u32[]{:S(2)}) copy-start(f32[768]{0:T(1024)} %param.17) | copy-start | bytes 9220
  10.4 3.2 %copy-start = (bf16[256,768]{1,0:T(8,128)(2,1)S(1)}, bf16[256,768]{1,0:T(8,128)(2,1)}, u32[]{:S(2)}) copy-start(bf16[256,768]{1,0:T(8,128)(2,1)} %c_ref.1) | copy-start | bytes 1179652
  71.5 1.2 copy-start.1
  72.6 4.7 %copy-start.19 = (f32[576]{0:T(1024)S(1)}, f32[576]{0:T(1024)}, u32[]{:S(2)}) copy-start(f32[576]{0:T(1024)} %param.19) | copy-start | bytes 6916
  72.6 4.7 %copy-start.2 = (bf16[4,256,768]{2,1,0:T(8,128)(2,1)S(1)}, bf16[4,256,768]{2,1,0:T(8,128)(2,1)}, u32[]{:S(2)}) copy-start(bf16[4,256,768]{2,1,0:T(8,128)(2,1)} %copy-done.1) | copy-start | bytes 4718596
  111.0 3.3 %copy-start.20 = (f32[768]{0:T(1024)S(1)}, f32[768]{0:T(1024)}, u32[]{:S(2)}) copy-start(f32[768]{0:T(1024)} %param.23) | copy-start | bytes 9220
  114.3 4.1 %copy-start.23 = (bf16[1024,768]{1,0:T(8,128)(2,1)}, bf16[1024,768]{1,0:T(8,128)(2,1)S(1)}, u32[]{:S(2)}) copy-start(bf16[1024,768]{1,0:T(8,128)(2,1)S(1)} %get-tuple-element.85) | copy-start | bytes 4718596
  118.4 2.5 %copy-start.21 = (bf16[1024,768]{1,0:T(8,128)(2,1)}, bf16[1024,768]{1,0:T(8,128)(2,1)S(1)}, u32[]{:S(2)}) copy-start(bf16[1024,768]{1,0:T(8,128)(2,1)S(1)} %get-tuple-element.88) | copy-start | bytes 4718596
  120.9 2.7 %copy-start.14 = (f32[1,768]{1,0:T(1,128)S(1)}, f32[1,768]{1,0:T(1,128)}, u32[]{:S(2)}) copy-start(f32[1,768]{1,0:T(1,128)} %broadcast_in_dim.47) | copy-start | bytes 9220
  124.8 3.3 %copy-start.5 = (bf16[1024,192]{1,0:T(8,128)(2,1)S(1)}, bf16[1024,192]{1,0:T(8,128)(2,1)}, u32[]{:S(2)}) copy-start(bf16[1024,192]{1,0:T(8,128)(2,1)} %get-tuple-element.29) | copy-start | bytes 1179652
  124.8 3.3 %copy-start.9 = (bf16[8,96,2304]{2,1,0:T(8,128)(2,1)S(1)}, bf16[8,96,2304]{2,1,0:T(8,128)(2,1)}, u32[]{:S(2)}) copy-start(bf16[8,96,2304]{2,1,0:T(8,128)(2,1)} %get-tuple-element.27) | copy-start | bytes 10616836
  128.2 1.9 copy-start.22
  130.1 1.4 copy-start.18
  134.1 72.5 %copy-start.4 = (bf16[256,768]{1,0:T(8,128)(2,1)S(1)}, bf16[256,768]{1,0:T(8,128)(2,1)}, u32[]{:S(2)}) copy-start(bf16[256,768]{1,0:T(8,128)(2,1)} %param.13) | copy-start | bytes 1179652
  134.1 74.0 %copy-start.16 = (f32[768]{0:T(1024)S(1)}, f32[768]{0:T(1024)}, u32[]{:S(2)}) copy-start(f32[768]{0:T(1024)} %param.25) | copy-start | bytes 9220
  134.1 74.0 %copy-start.17 = (f32[768]{0:T(1024)S(1)}, f32[768]{0:T(1024)}, u32[]{:S(2)}) copy-start(f32[768]{0:T(1024)} %param.21) | copy-start | bytes 9220
  208.1 6.3 %copy-start.10 = (f32[96,192]{1,0:T(8,128)S(1)}, f32[96,192]{1,0:T(8,128)}, u32[]{:S(2)}) copy-start(f32[96,192]{1,0:T(8,128)} %get-tuple-element.35) | copy-start | bytes 221188
  208.1 7.6 %copy-start.8 = (f32[96,576]{1,0:T(8,128)S(1)}, f32[96,576]{1,0:T(8,128)}, u32[]{:S(2)}) copy-start(f32[96,576]{1,0:T(8,128)} %get-tuple-element.137) | copy-start | bytes 663556
  208.1 8.3 %copy-start.7 = (f32[96,768]{1,0:T(8,128)S(1)}, f32[96,768]{1,0:T(8,128)}, u32[]{:S(2)}) copy-start(f32[96,768]{1,0:T(8,128)} %get-tuple-element.141) | copy-start | bytes 884740
  208.1 9.0 %copy-start.6 = (f32[96,768]{1,0:T(8,128)S(1)}, f32[96,768]{1,0:T(8,128)}, u32[]{:S(2)}) copy-start(f32[96,768]{1,0:T(8,128)} %get-tuple-element.37) | copy-start | bytes 884740
  213.1 4.7 %copy-start.13 = (f32[768]{0:T(1024)}, f32[768]{0:T(1024)S(1)}, u32[]{:S(2)}) copy-start(f32[768]{0:T(1024)S(1)} %get-tuple-element.140) | copy-start | bytes 9220

commit v4 on v3

--- a/solution.py
+++ b/solution.py
@@ -424,8 +424,11 @@
 
 def attention_kernel(
     heads,
-    x_ref,
-    do_ref,
+    f_ref,
+    c_ref,
+    wq_ref,
+    bq_ref,
+    wo_ref,
     cos_ref,
     sin_ref,
     turn_ref,
@@ -442,8 +445,10 @@
     grad_q,
     grad_k,
     grad_v,
+    x_ref,
+    do_ref,
 ):
-    length = x_ref.shape[0]
+    length = f_ref.shape[0]
     span = min(SPAN, length)
     scale = HEAD_DIM ** (-0.5)
     two = 2 * HEAD_DIM
@@ -459,6 +464,12 @@
             preferred_element_type=f32,
         )
 
+    for first in range(0, length, span):
+        part = slice(first, first + span)
+        x_ref[part] = (
+            jnp.dot(f_ref[part], wq_ref[...], preferred_element_type=f32) + bq_ref[...]
+        )
+        do_ref[part] = jnp.dot(c_ref[part], wo_ref[...], preferred_element_type=f32).astype(bf16)
     for n in range(heads):
         base = 3 * HEAD_DIM * n
         for first in range(0, length, span):
@@ -533,11 +544,7 @@
         -1.0,
         jnp.where((inner >= half) & (inner < ROT) & (source == target - half), 1.0, 0.0),
     ).astype(jnp.float32)
-    packed = jnp.dot(features, qkv_full, preferred_element_type=jnp.float32) + qkv_bias
-    mixed_grad = jnp.dot(grad_rows, out_full, preferred_element_type=jnp.float32).astype(
-        jnp.bfloat16
-    )
-    wide = packed.shape[1]
+    wide = qkv_full.shape[1]
     vmem = pl.BlockSpec(memory_space=pltpu.VMEM)
     mixed_rows, packed_grad, sums = pl.pallas_call(
         functools.partial(attention_kernel, heads),
@@ -546,13 +553,28 @@
             jax.ShapeDtypeStruct((length, wide), jnp.bfloat16),
             jax.ShapeDtypeStruct((1, wide), jnp.float32),
         ),
-        in_specs=[vmem] * 7,
+        in_specs=[vmem] * 10,
         out_specs=(vmem,) * 3,
         scratch_shapes=[pltpu.VMEM((heads, length, HEAD_DIM), jnp.bfloat16)] * 5
-        + [pltpu.VMEM((heads, length, HEAD_DIM), jnp.float32)] * 3,
+        + [pltpu.VMEM((heads, length, HEAD_DIM), jnp.float32)] * 3
+        + [
+            pltpu.VMEM((length, wide), jnp.float32),
+            pltpu.VMEM((length, heads * HEAD_DIM), jnp.bfloat16),
+        ],
         compiler_params=pltpu.CompilerParams(vmem_limit_bytes=56 * 1024 * 1024),
         name="attention",
-    )(packed, mixed_grad, cos_full, sin_full, turn, segment_row[:, None], segment_row[None, :])
+    )(
+        features,
+        grad_rows,
+        qkv_full,
+        qkv_bias[None],
+        out_full,
+        cos_full,
+        sin_full,
+        turn,
+        segment_row[:, None],
+        segment_row[None, :],
+    )
     return mixed_rows, packed_grad, sums[0]
 
 

time: 219 us -> 218 us (level)
  matrix products: 34.1 us -> 27.5 us
  local copies, waits for them, and re-layouts: 21.6 us -> 25.2 us
    dot_general x2 -> x0, matrix products: 6.74 us -> none  [the longest x1 4.1 us: attention_branch(): jnp.dot(features, qkv_full, preferred_element_type=jnp.float32) + qkv_bias]
    split x0 -> x2, local copies, waits for them, and re-layouts: none -> 4.26 us  [body(): full_up, full_down, full_qkv, full_out = jnp.split(w_all, ends, axis=1)]
    unnamed x54 -> x64, local copies, waits for them, and re-layouts: 5.6 us -> 6.79 us
where the time goes in v4:
time: 218 us; the launch traced here: 217 us
  Pallas kernels  151 us (69%)
  matrix products  27.5 us (13%)
  local copies, waits for them, and re-layouts  25.2 us (12%)
  other arithmetic  11.5 us (5%)
    pallas_call x1, Pallas kernels, scatter_all(): pl.pallas_call(functools.partial(scatter_kernel, fsdp, tp, many), out_sha...  72.5 us
    pallas_call x1, Pallas kernels, gather_all(): pl.pallas_call(functools.partial(gather_kernel, fsdp, tp), out_shape=shap...  57.8 us
    pallas_call x1, Pallas kernels, attention_branch(): pl.pallas_call(functools.partial(attention_kernel, heads), out_shape=(jax...  21 us
    dot_general x4, matrix products, cross_rows(): lax.dot_general(left, right, (((0,), (0,)), ((), ())), preferred_element_...  10.9 us
    dot_general x4, matrix products, cross_cols(): lax.dot_general(left, right, (((1,), (1,)), ((), ())), preferred_element_...  9.25 us
    unnamed x64, local copies, waits for them, and re-layouts  6.79 us

profile of v4, /device:TPU:0, one launch (start us, length us, event | category | flops | bytes accessed | tf_op | source)
XLA Modules:
  0.0 216.6 jit_solution(13545060506827829868)
XLA Ops:
  1.6 1.1 convert_reduce_fusion
  2.7 1.2 fusion.14
  4.0 1.3 broadcast_in_dim.24.bq_ref
  5.9 1.1 convert_reduce_fusion.1
  7.5 0.9 copy.29
  9.6 1.0 copy.31.sin_ref
  10.6 1.0 copy.30.cos_ref
  11.7 1.0 copy.32.col_ref
  12.7 1.1 fusion.12
  13.8 57.8 %gather_all.1 = (bf16[8,96,2304]{2,1,0:T(8,128)(2,1)}, bf16[4,256,768]{2,1,0:T(8,128)(2,1)S(1)}, bf16[4,256,768]{2,1,0:T(8,128)(2,1)S(1)}) custom-call(bf16[96,2304]{1,0:T(8,128)(2,1)S(1)} %concatenate.20.w_ref, bf16[256,768]{1,0:T(8,128)(2,1)S(1)} %get-tuple-element.68.h_ref, bf16[256,768]{1,0:T(8,128)(2,1)S(1)} %copy-done), custom_call_target="tpu_custom_call" | custom-call | tf_op jit(solution)/shard_map/gather_all/pallas_call | solution.py:189
  71.7 1.2 copy-done.1
  72.8 1.2 copy-done.3
  74.0 1.9 split.19.wo_ref
  75.9 2.3 %split.18.wq_ref = bf16[768,576]{1,0:T(8,128)(2,1)} slice(bf16[768,2304]{1,0:T(8,128)(2,1)} %bitcast.55), slice={[0:768], [1536:2112]} | slice | bytes 1769472 | tf_op jit(solution)/shard_map/split | solution.py:607
  78.3 21.0 %attention.1 = (bf16[1024,192]{1,0:T(8,128)(2,1)}, bf16[1024,576]{1,0:T(8,128)(2,1)}, f32[1,576]{1,0:T(1,128)}) custom-call(bf16[1024,768]{1,0:T(8,128)(2,1)} %bitcast.38, bf16[1024,768]{1,0:T(8,128)(2,1)} %bitcast.42, bf16[768,576]{1,0:T(8,128)(2,1)} %split.18.wq_ref, f32[1,576]{1,0:T(1,128)} %broadcast_in_dim.24.bq_ref, bf16[768,192]{1,0:T(8,128)(2,1)} %split.19.wo_ref, ...), custom_call_target="tpu_custom_call" | custom-call | tf_op jit(solution)/shard_map/attention/pallas_call | solution.py:549
  100.0 2.4 %convolution_convert_fusion.3 = bf16[768,192]{0,1:T(8,128)(2,1)} fusion(bf16[1024,768]{1,0:T(8,128)(2,1)S(1)} %bitcast.43, bf16[1024,192]{1,0:T(8,128)(2,1)} %get-tuple-element.29), kind=kOutput, calls=%fused_computation.13 | convolution fusion | flops 302137344 | bytes 2260992 | tf_op jit(solution)/shard_map/dot_general | solution.py:60
  102.4 1.9 copy.34
  104.3 3.5 %convolution_convert_fusion.2 = bf16[768,576]{0,1:T(8,128)(2,1)} fusion(bf16[1024,768]{1,0:T(8,128)(2,1)S(1)} %bitcast.39, bf16[1024,576]{1,0:T(8,128)(2,1)} %get-tuple-element.28), kind=kOutput, calls=%fused_computation.12 | convolution fusion | flops 906412032 | bytes 3637248 | tf_op jit(solution)/shard_map/dot_general | solution.py:60
  107.8 2.2 %copy.33 = bf16[768,576]{1,0:T(8,128)(2,1)} copy(bf16[768,576]{0,1:T(8,128)(2,1)} %convolution_convert_fusion.2) | data formatting | bytes 1769472 | tf_op jit(solution)/shard_map/convert_element_type | solution.py:624
  110.0 3.2 %multiply_convert_fusion = (bf16[1024,768]{1,0:T(8,128)(2,1)S(1)}, f32[1024,768]{1,0:T(8,128)S(1)}) fusion(f32[768]{0:T(1024)} %param.23, bf16[1024,768]{1,0:T(8,128)(2,1)S(1)} %bitcast.40, bf16[768,2304]{1,0:T(8,128)(2,1)} %bitcast.56), kind=kOutput, calls=%fused_computation.8 | convolution fusion | flops 1212678144 | bytes 7475200 | tf_op jit(solution)/shard_map/dot_general | solution.py:609
  113.3 4.1 %fusion.26 = (f32[768]{0:T(1024)S(1)}, bf16[1024,768]{1,0:T(8,128)(2,1)S(1)}) fusion(f32[1024,768]{1,0:T(8,128)S(1)} %get-tuple-element.74, f32[768]{0:T(1024)S(1)} %copy-done.25, bf16[1024,768]{1,0:T(8,128)(2,1)S(1)} %bitcast.44, bf16[768,2304]{1,0:T(8,128)(2,1)} %bitcast.57), kind=kOutput, calls=%fused_computation.71 | convolution fusion | flops 1217395968 | bytes 7477248 | tf_op jit(solution)/shard_map/dot_general | solution.py:611
  117.4 2.4 %convolution_convert_fusion = bf16[768,768]{1,0:T(8,128)(2,1)} fusion(bf16[1024,768]{1,0:T(8,128)(2,1)S(1)} %bitcast.45, bf16[1024,768]{1,0:T(8,128)(2,1)S(1)} %get-tuple-element.73), kind=kOutput, calls=%fused_computation.10 | convolution fusion | flops 1208549376 | bytes 4325376 | tf_op jit(solution)/shard_map/dot_general | solution.py:60
  119.8 2.6 %convolution_convert_fusion.1 = bf16[768,768]{1,0:T(8,128)(2,1)} fusion(bf16[1024,768]{1,0:T(8,128)(2,1)S(1)} %bitcast.41, bf16[1024,768]{1,0:T(8,128)(2,1)S(1)} %get-tuple-element.76), kind=kOutput, calls=%fused_computation.11 | convolution fusion | flops 1208549376 | bytes 4325376 | tf_op jit(solution)/shard_map/dot_general | solution.py:60
  122.5 1.3 concatenate.26.refs_7_
  123.8 3.3 %fusion.9 = f32[1024,768]{1,0:T(8,128)S(1)} fusion(bf16[1024,768]{1,0:T(8,128)(2,1)} %copy-done.28, bf16[768,2304]{1,0:T(8,128)(2,1)} %bitcast.58), kind=kOutput, calls=%fused_computation.21 | convolution fusion | flops 1207959552 | bytes 5898240 | tf_op jit(solution)/shard_map/dot_general | solution.py:66
  127.1 1.9 add_convert_fusion.1
  129.0 1.4 fusion.5
  130.5 2.6 %add_convert_fusion = bf16[1024,768]{1,0:T(8,128)(2,1)} fusion(f32[1024,768]{1,0:T(8,128)S(1)} %fusion.5, bf16[1024,576]{1,0:T(8,128)(2,1)S(1)} %copy-done.24, bf16[768,2304]{1,0:T(8,128)(2,1)S(1)} %bitcast.61), kind=kOutput, calls=%fused_computation.6 | convolution fusion | flops 907542528 | bytes 7012352 | tf_op jit(solution)/shard_map/dot_general | solution.py:66
  133.1 72.5 %scatter_all.1 = (f32[96,768]{1,0:T(8,128)}, f32[96,768]{1,0:T(8,128)}, f32[96,576]{1,0:T(8,128)}, f32[96,192]{1,0:T(8,128)}, f32[256,768]{1,0:T(8,128)}, /*index=5*/f32[256,768]{1,0:T(8,128)}, f32[16,768]{1,0:T(8,128)}) custom-call(bf16[8,96,768]{2,1,0:T(8,128)(2,1)} %bitcast.53, bf16[8,96,768]{2,1,0:T(8,128)(2,1)} %bitcast.52, ...), custom_call_target="tpu_custom_call" | custom-call | tf_op jit(solution)/shard_map/scatter_all/pallas_call | solution.py:382
  205.6 1.5 multiply_reduce_fusion.1
  207.2 2.4 %fusion.15 = (bf16[256,768]{1,0:T(8,128)(2,1)}, bf16[256,768]{1,0:T(8,128)(2,1)}) fusion(bf16[256,768]{1,0:T(8,128)(2,1)S(1)} %copy-done, f32[256,768]{1,0:T(8,128)S(1)} %copy-done.7, f32[256]{0:T(256)S(1)} %broadcast_multiply_fusion, f32[256]{0:T(256)S(1)} %broadcast_multiply_fusion.1, f32[768]{0:T(1024)S(1)} %copy-done.18, f32[256]{0:T(256)S(1)} %add_rsqrt_fusion, ...), kind=kLoop, calls=%fused_computation.29 | loop fusion | flops 2949120 | bytes 3159040 | tf_op jit(solution)/shard_map/convert_element_type | solution.py:662
  210.4 1.5 slice_reduce_fusion.1
  (92 shorter events, 9.6 us)
Async XLA Ops:
  0.6 8.7 %copy-start.14 = (bf16[768,96]{0,1:T(8,128)(2,1)S(1)}, bf16[768,96]{0,1:T(8,128)(2,1)}, u32[]{:S(2)}) copy-start(bf16[768,96]{0,1:T(8,128)(2,1)} %param.24) | copy-start | bytes 442372
  0.7 8.7 %copy-start.13 = (bf16[96,768]{1,0:T(8,128)(2,1)S(1)}, bf16[96,768]{1,0:T(8,128)(2,1)}, u32[]{:S(2)}) copy-start(bf16[96,768]{1,0:T(8,128)(2,1)} %param.22) | copy-start | bytes 442372
  0.7 8.6 %copy-start.15 = (bf16[96,576]{1,0:T(8,128)(2,1)S(1)}, bf16[96,576]{1,0:T(8,128)(2,1)}, u32[]{:S(2)}) copy-start(bf16[96,576]{1,0:T(8,128)(2,1)} %param.18) | copy-start | bytes 331780
  9.5 2.1 copy-start.17
  9.5 3.1 %copy-start.5 = (bf16[256,768]{1,0:T(8,128)(2,1)S(1)}, bf16[256,768]{1,0:T(8,128)(2,1)}, u32[]{:S(2)}) copy-start(bf16[256,768]{1,0:T(8,128)(2,1)} %param.13) | copy-start | bytes 1179652
  9.5 3.1 %copy-start.18 = (f32[768]{0:T(1024)S(1)}, f32[768]{0:T(1024)}, u32[]{:S(2)}) copy-start(f32[768]{0:T(1024)} %param.16) | copy-start | bytes 9220
  9.5 3.1 %copy-start.21 = (f32[768]{0:T(1024)S(1)}, f32[768]{0:T(1024)}, u32[]{:S(2)}) copy-start(f32[768]{0:T(1024)} %param.17) | copy-start | bytes 9220
  10.6 3.2 %copy-start = (bf16[256,768]{1,0:T(8,128)(2,1)S(1)}, bf16[256,768]{1,0:T(8,128)(2,1)}, u32[]{:S(2)}) copy-start(bf16[256,768]{1,0:T(8,128)(2,1)} %c_ref.1) | copy-start | bytes 1179652
  71.6 1.2 copy-start.1
  72.8 1.2 copy-start.3
  78.3 21.7 %copy-start.4 = (bf16[4,256,768]{2,1,0:T(8,128)(2,1)S(1)}, bf16[4,256,768]{2,1,0:T(8,128)(2,1)}, u32[]{:S(2)}) copy-start(bf16[4,256,768]{2,1,0:T(8,128)(2,1)} %copy-done.3) | copy-start | bytes 4718596
  100.0 4.3 %copy-start.2 = (bf16[4,256,768]{2,1,0:T(8,128)(2,1)S(1)}, bf16[4,256,768]{2,1,0:T(8,128)(2,1)}, u32[]{:S(2)}) copy-start(bf16[4,256,768]{2,1,0:T(8,128)(2,1)} %copy-done.1) | copy-start | bytes 4718596
  110.0 3.3 %copy-start.25 = (f32[768]{0:T(1024)S(1)}, f32[768]{0:T(1024)}, u32[]{:S(2)}) copy-start(f32[768]{0:T(1024)} %param.23) | copy-start | bytes 9220
  113.2 4.1 %copy-start.28 = (bf16[1024,768]{1,0:T(8,128)(2,1)}, bf16[1024,768]{1,0:T(8,128)(2,1)S(1)}, u32[]{:S(2)}) copy-start(bf16[1024,768]{1,0:T(8,128)(2,1)S(1)} %get-tuple-element.73) | copy-start | bytes 4718596
  117.4 2.5 %copy-start.26 = (bf16[1024,768]{1,0:T(8,128)(2,1)}, bf16[1024,768]{1,0:T(8,128)(2,1)S(1)}, u32[]{:S(2)}) copy-start(bf16[1024,768]{1,0:T(8,128)(2,1)S(1)} %get-tuple-element.76) | copy-start | bytes 4718596
  119.8 2.7 %copy-start.20 = (f32[1,768]{1,0:T(1,128)S(1)}, f32[1,768]{1,0:T(1,128)}, u32[]{:S(2)}) copy-start(f32[1,768]{1,0:T(1,128)} %broadcast_in_dim.50) | copy-start | bytes 9220
  123.8 3.3 %copy-start.8 = (bf16[8,96,2304]{2,1,0:T(8,128)(2,1)S(1)}, bf16[8,96,2304]{2,1,0:T(8,128)(2,1)}, u32[]{:S(2)}) copy-start(bf16[8,96,2304]{2,1,0:T(8,128)(2,1)} %get-tuple-element.27) | copy-start | bytes 10616836
  123.8 3.3 %copy-start.9 = (bf16[1024,192]{1,0:T(8,128)(2,1)S(1)}, bf16[1024,192]{1,0:T(8,128)(2,1)}, u32[]{:S(2)}) copy-start(bf16[1024,192]{1,0:T(8,128)(2,1)} %get-tuple-element.29) | copy-start | bytes 1179652
  127.1 1.9 copy-start.27
  129.0 1.4 copy-start.24
  133.1 72.5 %copy-start.6 = (bf16[256,768]{1,0:T(8,128)(2,1)S(1)}, bf16[256,768]{1,0:T(8,128)(2,1)}, u32[]{:S(2)}) copy-start(bf16[256,768]{1,0:T(8,128)(2,1)} %param.13) | copy-start | bytes 1179652
  133.1 74.1 %copy-start.22 = (f32[768]{0:T(1024)S(1)}, f32[768]{0:T(1024)}, u32[]{:S(2)}) copy-start(f32[768]{0:T(1024)} %param.25) | copy-start | bytes 9220
  133.1 74.1 %copy-start.23 = (f32[768]{0:T(1024)S(1)}, f32[768]{0:T(1024)}, u32[]{:S(2)}) copy-start(f32[768]{0:T(1024)} %param.21) | copy-start | bytes 9220
  205.6 1.6 copy-start.7
  207.2 6.0 %copy-start.16 = (f32[96,192]{1,0:T(8,128)S(1)}, f32[96,192]{1,0:T(8,128)}, u32[]{:S(2)}) copy-start(f32[96,192]{1,0:T(8,128)} %get-tuple-element.35) | copy-start | bytes 221188
  207.2 7.3 %copy-start.12 = (f32[96,576]{1,0:T(8,128)S(1)}, f32[96,576]{1,0:T(8,128)}, u32[]{:S(2)}) copy-start(f32[96,576]{1,0:T(8,128)} %get-tuple-element.125) | copy-start | bytes 663556
  207.2 8.0 %copy-start.11 = (f32[96,768]{1,0:T(8,128)S(1)}, f32[96,768]{1,0:T(8,128)}, u32[]{:S(2)}) copy-start(f32[96,768]{1,0:T(8,128)} %get-tuple-element.129) | copy-start | bytes 884740
  207.2 8.7 %copy-start.10 = (f32[96,768]{1,0:T(8,128)S(1)}, f32[96,768]{1,0:T(8,128)}, u32[]{:S(2)}) copy-start(f32[96,768]{1,0:T(8,128)} %get-tuple-element.37) | copy-start | bytes 884740
  211.9 4.7 %copy-start.19 = (f32[768]{0:T(1024)}, f32[768]{0:T(1024)S(1)}, u32[]{:S(2)}) copy-start(f32[768]{0:T(1024)S(1)} %get-tuple-element.128) | copy-start | bytes 9220
